TPU v7x, 128 devices: a whole 4x4x4 slice. The times are simulated.
128 devices in a mesh: gx: 8 (over z, core), gy: 16 (over x, y).
Axes of the slice: x: 4, y: 4, z: 4, core: 2. Of those that a mesh axis runs over, the one named last changes fastest.
Arguments:
- initial_state: float32 [2, 32, 48, 2048], P(None, 'gx', None, 'gy'), may hold values from -6 to 6
- eddy_diffusivity: float32 [32, 48, 2048], P('gx', None, 'gy'), may hold values from 0.02 to 0.12
- velocity: float32 [3, 32, 48, 2048], P(None, 'gx', None, 'gy'), may hold values from -0.08 to 0.08
- target: float32 [2, 32, 48, 2048], P(None, 'gx', None, 'gy'), may hold values from -6 to 6
- sensor_cell: int32 [32768], P(('gx', 'gy')), may hold values from 0 to 24575
- sensor_owner: int32 [32768, 1], P(('gx', 'gy')), may hold values from 0 to 127; in each aligned block of 256 rows (0 to 255, 256 to 511, ...) at most 4 rows name the same one
- observations: float32 [32768, 2, 4], P(('gx', 'gy')), may hold values from -6 to 6
- actuator_block: int32 [4096], P(('gx', 'gy')), may hold values from 0 to 191
- actuator_owner: int32 [4096, 1], P(('gx', 'gy')), may hold values from 0 to 15; in each aligned block of 32 rows (0 to 31, 32 to 63, ...) at most 4 rows name the same one
- controls: float32 [4096, 2], P(('gx', 'gy')), may hold values from -6 to 6
- footprint: float32 [4096, 128], P(('gx', 'gy')), may hold values from 0 to 1
Outputs:
- final_state: float32 [2, 32, 48, 2048], P(None, 'gx', None, 'gy')
- initial_sensitivity: float32 [2, 32, 48, 2048], P(None, 'gx', None, 'gy')
- actuator_gradient: float32 [4096, 2], P(('gx', 'gy'))
Inputs may be any that keep to these rules, and one draw needn't show every extreme that they name: `sensor_owner`: among the 256 rows of one device, no owner is named more than 4 times, a bound that some block reaches. `actuator_owner`: among the 32 rows of one device, no owner is named more than 4 times, a bound that some block reaches.
All inputs are finite; a program needn't handle non-finite values.
Results may differ from a plain program's by a relative error of at most 0.00002.
Values sent between devices are 32-bit elements; how exact they have to be, the bound alone decides.
A program may use at most 128 MiB of HBM per device.

v0:
```python
import functools

import jax
import jax.numpy as jnp
from jax import lax
from jax.experimental import pallas as pl
from jax.experimental.pallas import tpu as pltpu
from jax.sharding import PartitionSpec as P

MESH = pl.DeviceIdType.MESH
F32 = jnp.float32
BF16 = jnp.bfloat16
HIGH = lax.Precision.HIGHEST

CX = 4
NZ = 48
CY = 128
FX = 4
FZ = 8
FY = 4
BZ = NZ // FZ
STEPS = 4
ZV = NZ // 8
PZ = NZ + 16
Z0 = 8
prandtl = 0.85
SCALES = (1.0, 1.0 / prandtl)


def iota(shape, dim):
    return lax.broadcasted_iota(jnp.int32, shape, dim)


def dot_nn(a, b, precision=None):
    return lax.dot_general(
        a, b, (((1,), (0,)), ((), ())), precision=precision, preferred_element_type=F32
    )


def dot_nt(a, b, precision=None):
    return lax.dot_general(
        a, b, (((1,), (1,)), ((), ())), precision=precision, preferred_element_type=F32
    )


def split3(x):
    hi = x.astype(BF16)
    rest = x - hi.astype(F32)
    mid = rest.astype(BF16)
    low = (rest - mid.astype(F32)).astype(BF16)
    return hi, mid, low


def rank_of(onehot):
    count = onehot.shape[1]
    earlier = (iota((count, count), 0) < iota((count, count), 1)).astype(F32)
    before = dot_nn(onehot, earlier)
    return jnp.sum(onehot * before, axis=0, keepdims=True).astype(jnp.int32)


def pack_edges(planes):
    lane = iota((8, CY), 1)
    packed = jnp.zeros((8, CY), F32)
    for zv in range(ZV):
        for p, plane in enumerate(planes):
            q = zv * len(planes) + p
            turned = pltpu.roll(plane[zv * 8 : zv * 8 + 8], 2 * q + 1, 1)
            packed = jnp.where(lax.shift_right_logical(lane, 1) == q, turned, packed)
    return packed


def unpack_edges(left, right, number):
    lane = iota((8, CY), 1)
    both = jnp.where((lane & 1) == 0, pltpu.roll(right, CY - 1, 1), pltpu.roll(left, 1, 1))
    planes = []
    for p in range(number):
        parts = [
            pltpu.roll(both, CY - (2 * (zv * number + p) + 1), 1) for zv in range(ZV)
        ]
        planes.append(jnp.concatenate(parts, axis=0))
    return planes


def beside_y(plane, halo):
    lane = iota(plane.shape, 1)
    above = jnp.where(lane == CY - 1, halo, pltpu.roll(plane, CY - 1, 1))
    below = jnp.where(lane == 0, halo, pltpu.roll(plane, 1, 1))
    return above, below


def whole_kernel(
    gxn,
    gyn,
    c0_h,
    kap_h,
    vel_h,
    tgt_h,
    cell_r,
    own_r,
    obs_r,
    ablk_r,
    aown_r,
    ctl_r,
    foot_r,
    out_c,
    out_s,
    out_g,
    fields,
    kap,
    velx,
    velyz,
    tgt,
    cof_f,
    cof_a,
    src,
    cnt,
    obsf,
    summed,
    act_o,
    act_i,
    sen_o,
    sen_i,
    sn2_o,
    sn2_i,
    edge_o,
    edge_l,
    edge_r,
    grad_o,
    grad_i,
    loc_sem,
    xs_sem,
    xr_sem,
    es_sem,
    er_sem,
    as_sem,
    ar_sem,
    ss_sem,
    sr_sem,
    ts_sem,
    tr_sem,
    gs_sem,
    gr_sem,
):
    me_x = lax.axis_index("gx")
    me_y = lax.axis_index("gy")
    lg_y = gyn.bit_length() - 1
    mid = slice(Z0, Z0 + NZ)

    loads = [
        pltpu.make_async_copy(c0_h, fields.at[0, :, 1 : 1 + CX, mid, :], loc_sem.at[0]),
        pltpu.make_async_copy(kap_h, kap.at[1 : 1 + CX, mid, :], loc_sem.at[1]),
        pltpu.make_async_copy(vel_h.at[0], velx.at[1 : 1 + CX, mid, :], loc_sem.at[2]),
        pltpu.make_async_copy(vel_h.at[1:3], velyz.at[:, :, mid, :], loc_sem.at[3]),
        pltpu.make_async_copy(tgt_h, tgt, loc_sem.at[4]),
    ]
    for load in loads:
        load.start()

    barrier = pltpu.get_barrier_semaphore()

    @pl.loop(1, gyn)
    def _(t):
        pl.semaphore_signal(
            barrier, inc=1, device_id=(me_x, lax.rem(me_y + t, gyn)), device_id_type=MESH
        )

    @pl.loop(1, gxn)
    def _(t):
        pl.semaphore_signal(
            barrier, inc=1, device_id=(lax.rem(me_x + t, gxn), me_y), device_id_type=MESH
        )

    rows = gyn * 8
    acts = aown_r.shape[1]
    aown = aown_r[...]
    slot_row = iota((rows, acts), 0)
    arank = rank_of((iota((gyn, acts), 0) == aown).astype(F32))
    to_tile = lax.shift_right_logical(slot_row, 3) == aown
    pick_foot = (to_tile & ((slot_row & 7) == arank)).astype(F32)
    pick_meta = (to_tile & ((slot_row & 7) == arank + 4)).astype(F32)
    meta_row = iota((CY, acts), 0)
    meta = jnp.where(
        meta_row == 0,
        ablk_r[...].astype(F32) + 1.0,
        jnp.where(
            meta_row == 1, ctl_r[0:1, :], jnp.where(meta_row == 2, ctl_r[1:2, :], 0.0)
        ),
    )
    act_o[...] = dot_nn(pick_foot, foot_r[...], HIGH) + dot_nt(pick_meta, meta, HIGH)

    sens = own_r.shape[1]
    owner = own_r[...]
    spot = (owner & (gyn - 1)) * 8 + lax.shift_right_logical(owner, lg_y)
    pick_sens = (iota((rows, sens), 0) == spot).astype(F32)
    srank = rank_of(pick_sens)
    datum = jnp.concatenate(
        [
            cell_r[...].astype(F32) + 1.0,
            obs_r[0],
            obs_r[1],
            jnp.zeros((7, sens), F32),
        ],
        axis=0,
    )
    spread = [jnp.where(srank == k, datum, 0.0) for k in range(4)]
    spread.append(jnp.zeros((64, sens), F32))
    sen_o[...] = dot_nt(pick_sens, jnp.concatenate(spread, axis=0), HIGH)

    zero_rows = jnp.zeros((8, CY), F32)
    for slot in range(8):
        for s in range(2):
            for x in range(1, 1 + CX):
                fields[slot, s, x, 0:8, :] = zero_rows
                fields[slot, s, x, Z0 + NZ : PZ, :] = zero_rows
    for x in range(1, 1 + CX):
        kap[x, 0:8, :] = zero_rows
        kap[x, Z0 + NZ : PZ, :] = zero_rows
        velyz[1, x - 1, 0:8, :] = zero_rows
        velyz[1, x - 1, Z0 + NZ : PZ, :] = zero_rows
    zero_plane = jnp.zeros((NZ, CY), F32)

    def zero_side(x):
        for slot in range(8):
            for s in range(2):
                fields[slot, s, x, mid, :] = zero_plane
        kap[x, mid, :] = zero_plane
        velx[x, mid, :] = zero_plane

    @pl.when(me_x == 0)
    def _():
        zero_side(0)

    @pl.when(me_x == gxn - 1)
    def _():
        zero_side(CX + 1)

    @pl.when(me_y == 0)
    def _():
        edge_l[...] = jnp.zeros_like(edge_l)

    @pl.when(me_y == gyn - 1)
    def _():
        edge_r[...] = jnp.zeros_like(edge_r)

    for load in loads[:4]:
        load.wait()

    state_planes = [fields[0, s, 1 + x, mid, :] for s in range(2) for x in range(CX)]
    edge_o[0] = pack_edges(state_planes)
    coef_planes = [kap[1 + x, mid, :] for x in range(CX)]
    coef_planes += [velyz[0, x, mid, :] for x in range(CX)]
    edge_o[8] = pack_edges(coef_planes)

    pl.semaphore_wait(barrier, gyn - 1 + gxn - 1)

    def to_peer_y(source, sink, send, recv):
        def make(t):
            there = lax.rem(me_y + t, gyn)
            return pltpu.make_async_remote_copy(
                src_ref=source(there),
                dst_ref=sink(me_y),
                send_sem=send.at[t],
                recv_sem=recv.at[t],
                device_id=(me_x, there),
                device_id_type=MESH,
            )

        return make

    def of_peer_y(source, sink, send, recv):
        def make(t):
            there = lax.rem(me_y + gyn - t, gyn)
            return pltpu.make_async_remote_copy(
                src_ref=source(there),
                dst_ref=sink(there),
                send_sem=send.at[t],
                recv_sem=recv.at[t],
                device_id=(me_x, there),
                device_id_type=MESH,
            )

        return make

    def tile_of(ref):
        return lambda d: ref.at[pl.ds(pl.multiple_of(d * 8, 8), 8), :]

    act_to = to_peer_y(tile_of(act_o), tile_of(act_i), as_sem, ar_sem)
    act_of = of_peer_y(tile_of(act_o), tile_of(act_i), as_sem, ar_sem)
    sen_to = to_peer_y(tile_of(sen_o), tile_of(sen_i), ss_sem, sr_sem)
    sen_of = of_peer_y(tile_of(sen_o), tile_of(sen_i), ss_sem, sr_sem)
    same = lambda d: grad_o
    grad_to = to_peer_y(same, tile_of(grad_i), gs_sem, gr_sem)
    grad_of = of_peer_y(same, tile_of(grad_i), gs_sem, gr_sem)

    def edge_copy(slot, side):
        there = me_y - 1 if side == 0 else me_y + 1
        sink = edge_r if side == 0 else edge_l
        return pltpu.make_async_remote_copy(
            src_ref=edge_o.at[slot],
            dst_ref=sink.at[slot],
            send_sem=es_sem.at[slot, side],
            recv_sem=er_sem.at[slot, side],
            device_id=(me_x, there),
            device_id_type=MESH,
        )

    def x_copy(slot, side):
        there = me_x - 1 if side == 0 else me_x + 1
        sink = CX + 1 if side == 0 else 0
        own = 0 if side == 0 else CX - 1
        if slot == 0:
            source = c0_h.at[:, own]
            dest = fields.at[0, :, sink, mid, :]
        elif slot < 8:
            source = fields.at[slot, :, own + 1, mid, :]
            dest = fields.at[slot, :, sink, mid, :]
        elif slot == 8:
            source = kap_h.at[own]
            dest = kap.at[sink, mid, :]
        else:
            source = vel_h.at[0, own]
            dest = velx.at[sink, mid, :]
        return pltpu.make_async_remote_copy(
            src_ref=source,
            dst_ref=dest,
            send_sem=xs_sem.at[slot, side],
            recv_sem=xr_sem.at[slot, side],
            device_id=(there, me_y),
            device_id_type=MESH,
        )

    has = (
        (me_x > 0, me_x < gxn - 1),
        (me_y > 0, me_y < gyn - 1),
    )

    def both_sides(maker, axis, action, slots):
        for side in (0, 1):

            @pl.when(has[axis][side])
            def _(side=side):
                for slot in slots:
                    action(maker(slot, side))

    def start(copy):
        copy.start()

    def wait_send(copy):
        copy.wait_send()

    def wait_recv_x(slots):
        for side in (0, 1):

            @pl.when(has[0][1 - side])
            def _(side=side):
                for slot in slots:
                    x_copy(slot, side).wait_recv()

    def wait_recv_e(slots):
        for side in (0, 1):

            @pl.when(has[1][1 - side])
            def _(side=side):
                for slot in slots:
                    edge_copy(slot, side).wait_recv()

    @pl.loop(1, gyn)
    def _(t):
        act_to(t).start()

    both_sides(edge_copy, 1, start, (8, 0))
    both_sides(x_copy, 0, start, (8, 9, 0))

    @pl.loop(1, gyn)
    def _(t):
        sen_to(t).start()

    own_tile = pl.ds(pl.multiple_of(me_y * 8, 8), 8)
    act_i[own_tile, :] = act_o[own_tile, :]
    sen_i[own_tile, :] = sen_o[own_tile, :]

    wait_recv_x((8, 9))
    wait_recv_e((8,))
    halos = unpack_edges(edge_l[8], edge_r[8], 2 * CX)
    for x in range(CX):
        here = kap[1 + x, mid, :]
        kyp, kym = beside_y(here, halos[x])
        around = (
            kap[2 + x, mid, :],
            kap[x, mid, :],
            kyp,
            kym,
            kap[1 + x, Z0 + 1 : Z0 + NZ + 1, :],
            kap[1 + x, Z0 - 1 : Z0 + NZ - 1, :],
        )
        faces = [0.5 * (here + other) for other in around]
        total = faces[0] + faces[1] + faces[2] + faces[3] + faces[4] + faces[5]
        uy = velyz[0, x, mid, :]
        uyp, uym = beside_y(uy, halos[CX + x])
        ux = velx[1 + x, mid, :]
        uz = velyz[1, x, mid, :]
        drift_f = (-0.5 * ux, 0.5 * ux, -0.5 * uy, 0.5 * uy, -0.5 * uz, 0.5 * uz)
        drift_a = (
            0.5 * velx[2 + x, mid, :],
            -0.5 * velx[x, mid, :],
            0.5 * uyp,
            -0.5 * uym,
            0.5 * velyz[1, x, Z0 + 1 : Z0 + NZ + 1, :],
            -0.5 * velyz[1, x, Z0 - 1 : Z0 + NZ - 1, :],
        )
        for s in range(2):
            scale = SCALES[s]
            cof_f[s, 6, x] = 1.0 - scale * total
            for f in range(6):
                scaled = faces[f] if s == 0 else scale * faces[f]
                cof_f[s, f, x] = scaled + drift_f[f]
                cof_a[s, f, x] = scaled + drift_a[f]

    def stencil(slot, cof, s, x, halo):
        here = fields[slot, s, 1 + x, mid, :]
        yp, ym = beside_y(here, halo)
        return (
            cof_f[s, 6, x] * here
            + cof[s, 0, x] * fields[slot, s, 2 + x, mid, :]
            + cof[s, 1, x] * fields[slot, s, x, mid, :]
            + cof[s, 2, x] * yp
            + cof[s, 3, x] * ym
            + cof[s, 4, x] * fields[slot, s, 1 + x, Z0 + 1 : Z0 + NZ + 1, :]
            + cof[s, 5, x] * fields[slot, s, 1 + x, Z0 - 1 : Z0 + NZ - 1, :]
        )

    def send_field(slot):
        planes = [fields[slot, s, 1 + x, mid, :] for s in range(2) for x in range(CX)]
        edge_o[slot] = pack_edges(planes)
        both_sides(edge_copy, 1, start, (slot,))
        both_sides(x_copy, 0, start, (slot,))

    def take_field(slot):
        wait_recv_x((slot,))
        wait_recv_e((slot,))
        return unpack_edges(edge_l[slot], edge_r[slot], 2 * CX)

    halos = take_field(0)
    for s in range(2):
        for x in range(CX):
            fields[1, s, 1 + x, mid, :] = stencil(0, cof_f, s, x, halos[s * CX + x])

    @pl.loop(1, gyn)
    def _(t):
        act_of(t).wait_recv()

    got = act_i[...]
    moved = pltpu.roll(got, rows - 4, 0)
    sel = (iota((8, CY), 0) == iota((8, CY), 1)).astype(F32)
    metas = dot_nt(sel, moved, HIGH)
    blk_row = (metas[0:1] + 0.5).astype(jnp.int32) - 1
    live_row = ((iota((1, rows), 1) & 7) < 4) & (blk_row >= 0)
    bz_row = jnp.where(live_row, lax.shift_right_arithmetic(blk_row, 5), -1)
    blk_col = (moved[:, 0:1] + 0.5).astype(jnp.int32) - 1
    live_col = ((iota((rows, 1), 0) & 7) < 4) & (blk_col >= 0)
    first_y = jnp.where(live_col, (blk_col & 31) * FY, -8)
    at_y = [(iota((rows, CY), 1) == first_y + fy).astype(F32) for fy in range(FY)]
    perm_row = iota((CY, CY), 0)
    perm = (
        iota((CY, CY), 1) == (perm_row & 31) * FY + lax.shift_right_logical(perm_row, 5)
    ).astype(F32)
    foot_t = dot_nt(perm, got, HIGH)
    weights = [
        jnp.where(bz_row == bz, metas[1 + s : 2 + s], 0.0)
        for s in range(2)
        for bz in range(BZ)
    ]
    placed = jnp.zeros((2 * BZ * 32, CY), F32)
    for fy in range(FY):
        part = foot_t[fy * 32 : fy * 32 + 32]
        left = jnp.concatenate([part * w for w in weights], axis=0)
        placed = placed + dot_nn(left, at_y[fy], HIGH)
    for s in range(2):
        for bz in range(BZ):
            for fx in range(FX):
                row = (s * BZ + bz) * 32 + fx * 8
                src[s, fx, bz * 8 : bz * 8 + 8, :] = placed[row : row + 8]

    for s in range(2):
        for x in range(CX):
            fields[1, s, 1 + x, mid, :] = fields[1, s, 1 + x, mid, :] + src[s, x]
    send_field(1)

    @pl.loop(1, gyn)
    def _(t):
        sen_of(t).wait_recv()

    for d in range(gxn):
        sn2_o[d] = sen_i[pl.ds(d, gyn, stride=8), :]

    def sn2_copy(t, sending):
        there = lax.rem(me_x + t, gxn) if sending else lax.rem(me_x + gxn - t, gxn)
        return pltpu.make_async_remote_copy(
            src_ref=sn2_o.at[there],
            dst_ref=sn2_i.at[me_x] if sending else sn2_i.at[there],
            send_sem=ts_sem.at[t],
            recv_sem=tr_sem.at[t],
            device_id=(there, me_y),
            device_id_type=MESH,
        )

    @pl.loop(1, gxn)
    def _(t):
        sn2_copy(t, True).start()

    sn2_i[me_x] = sn2_o[me_x]

    def step_forward(slot, sink):
        halos = take_field(slot)
        for s in range(2):
            for x in range(CX):
                sink(s, x, stencil(slot, cof_f, s, x, halos[s * CX + x]) + src[s, x])

    def into(slot):
        def put(s, x, value):
            fields[slot, s, 1 + x, mid, :] = value

        return put

    step_forward(1, into(2))
    send_field(2)

    @pl.loop(1, gxn)
    def _(t):
        sn2_copy(t, False).wait_recv()

    records = jnp.concatenate([sn2_i[d] for d in range(gxn)], axis=0)
    many = records.shape[0]
    sel = (iota((8, CY), 0) * 16 == iota((8, CY), 1)).astype(F32)
    cell_rows = (dot_nt(sel, records, HIGH) + 0.5).astype(jnp.int32) - 1
    zx = lax.shift_right_arithmetic(cell_rows, 7)
    pick_zx = jnp.concatenate(
        [(iota((CX * NZ, many), 0) == zx[k : k + 1]).astype(BF16) for k in range(4)], axis=1
    )
    at_lane = []
    for k in range(4):
        cell_col = (records[:, 16 * k : 16 * k + 1] + 0.5).astype(jnp.int32) - 1
        lane = jnp.where(cell_col >= 0, cell_col & (CY - 1), -1)
        at_lane.append(iota((many, CY), 1) == lane)
    cnt[...] = dot_nn(
        pick_zx, jnp.concatenate([a.astype(F32).astype(BF16) for a in at_lane], axis=0)
    )
    for ch in range(2 * STEPS):
        values = jnp.concatenate(
            [
                jnp.where(at_lane[k], records[:, 16 * k + 1 + ch : 16 * k + 2 + ch], 0.0)
                for k in range(4)
            ],
            axis=0,
        )
        hi, mid_part, low = split3(values)
        obsf[ch] = (dot_nn(pick_zx, hi) + dot_nn(pick_zx, mid_part)) + dot_nn(pick_zx, low)

    step_forward(2, into(3))
    send_field(3)

    def forcing(state, s, x, n):
        span = slice(x * NZ, x * NZ + NZ)
        return cnt[span] * state - obsf[s * STEPS + n - 1, span]

    loads[4].wait()

    def last(s, x, value):
        out_c[s, x] = value
        adj = value - tgt[s, x] + forcing(value, s, x, 4)
        fields[4, s, 1 + x, mid, :] = adj
        summed[s, x] = adj

    step_forward(3, last)
    send_field(4)

    for n in (3, 2, 1):
        slot = 7 - n
        halos = take_field(slot)
        for s in range(2):
            for x in range(CX):
                adj = stencil(slot, cof_a, s, x, halos[s * CX + x]) + forcing(
                    fields[n, s, 1 + x, mid, :], s, x, n
                )
                fields[slot + 1, s, 1 + x, mid, :] = adj
                summed[s, x] = summed[s, x] + adj
        send_field(slot + 1)

    stacked = jnp.concatenate(
        [
            summed[s, fx, bz * 8 : bz * 8 + 8, :]
            for s in range(2)
            for bz in range(BZ)
            for fx in range(FX)
        ],
        axis=0,
    )
    totals = [jnp.zeros((32, rows), F32) for _ in range(2)]
    picked = [dot_nt(stacked, at_y[fy], HIGH) for fy in range(FY)]
    for s in range(2):
        for bz in range(BZ):
            base = (s * BZ + bz) * 32
            part = jnp.zeros((32, rows), F32)
            for fy in range(FY):
                part = part + foot_t[fy * 32 : fy * 32 + 32] * picked[fy][base : base + 32]
            totals[s] = totals[s] + jnp.where(bz_row == bz, part, 0.0)
    sums = [jnp.sum(t, axis=0, keepdims=True) for t in totals]
    if rows < CY:
        sums = [jnp.concatenate([v, jnp.zeros((1, CY - rows), F32)], axis=1) for v in sums]
    grad_o[...] = jnp.concatenate(sums + [jnp.zeros((6, CY), F32)], axis=0)

    @pl.loop(1, gyn)
    def _(t):
        grad_to(t).start()

    grad_i[own_tile, :] = grad_o[...]

    halos = take_field(7)
    for s in range(2):
        for x in range(CX):
            out_s[s, x] = stencil(7, cof_a, s, x, halos[s * CX + x])

    @pl.loop(1, gyn)
    def _(t):
        grad_of(t).wait_recv()

    pick_lane = (iota((CY, acts), 0) == me_y * 8 + arank).astype(F32)
    brought = dot_nn(grad_i[...], pick_lane, HIGH)
    mine = jnp.where(to_tile, brought, 0.0)
    for s in range(2):
        out_g[s : s + 1, :] = jnp.sum(
            jnp.where((slot_row & 7) == s, mine, 0.0), axis=0, keepdims=True
        )

    both_sides(edge_copy, 1, wait_send, range(9))
    both_sides(x_copy, 0, wait_send, range(10))

    @pl.loop(1, gyn)
    def _(t):
        act_to(t).wait_send()
        sen_to(t).wait_send()
        grad_to(t).wait_send()

    @pl.loop(1, gxn)
    def _(t):
        sn2_copy(t, True).wait_send()


def per_device(
    gxn,
    gyn,
    initial_state,
    eddy_diffusivity,
    velocity,
    target,
    sensor_cell,
    sensor_owner,
    observations,
    actuator_block,
    actuator_owner,
    controls,
    footprint,
):
    sens = sensor_cell.shape[0]
    acts = actuator_block.shape[0]
    rows = gyn * 8
    hbm = pl.BlockSpec(memory_space=pl.ANY)
    vmem = pl.BlockSpec(memory_space=pltpu.VMEM)
    dma = pltpu.SemaphoreType.DMA
    big = jax.ShapeDtypeStruct((2, CX, NZ, CY), F32)
    state, sensitivity, gradient = pl.pallas_call(
        functools.partial(whole_kernel, gxn, gyn),
        out_shape=(big, big, jax.ShapeDtypeStruct((2, acts), F32)),
        in_specs=[hbm] * 4 + [vmem] * 7,
        out_specs=(vmem, vmem, vmem),
        scratch_shapes=[
            pltpu.VMEM((8, 2, CX + 2, PZ, CY), F32),
            pltpu.VMEM((CX + 2, PZ, CY), F32),
            pltpu.VMEM((CX + 2, PZ, CY), F32),
            pltpu.VMEM((2, CX, PZ, CY), F32),
            pltpu.VMEM((2, CX, NZ, CY), F32),
            pltpu.VMEM((2, 7, CX, NZ, CY), F32),
            pltpu.VMEM((2, 6, CX, NZ, CY), F32),
            pltpu.VMEM((2, CX, NZ, CY), F32),
            pltpu.VMEM((CX * NZ, CY), F32),
            pltpu.VMEM((2 * STEPS, CX * NZ, CY), F32),
            pltpu.VMEM((2, CX, NZ, CY), F32),
            pltpu.VMEM((rows, CY), F32),
            pltpu.VMEM((rows, CY), F32),
            pltpu.VMEM((rows, CY), F32),
            pltpu.VMEM((rows, CY), F32),
            pltpu.VMEM((gxn, gyn, CY), F32),
            pltpu.VMEM((gxn, gyn, CY), F32),
            pltpu.VMEM((9, 8, CY), F32),
            pltpu.VMEM((9, 8, CY), F32),
            pltpu.VMEM((9, 8, CY), F32),
            pltpu.VMEM((8, CY), F32),
            pltpu.VMEM((rows, CY), F32),
            dma((5,)),
            dma((10, 2)),
            dma((10, 2)),
            dma((9, 2)),
            dma((9, 2)),
            dma((gyn,)),
            dma((gyn,)),
            dma((gyn,)),
            dma((gyn,)),
            dma((gxn,)),
            dma((gxn,)),
            dma((gyn,)),
            dma((gyn,)),
        ],
        compiler_params=pltpu.CompilerParams(
            collective_id=0, has_side_effects=True, vmem_limit_bytes=48 * 1024 * 1024
        ),
        name="whole",
    )(
        initial_state,
        eddy_diffusivity,
        velocity,
        target,
        sensor_cell.reshape(1, sens),
        sensor_owner.reshape(1, sens),
        jnp.transpose(observations, (1, 2, 0)),
        actuator_block.reshape(1, acts),
        actuator_owner.reshape(1, acts),
        controls.T,
        footprint,
    )
    return state, sensitivity, gradient.T


def solution(mesh):
    in_specs = (
        P(None, "gx", None, "gy"),
        P("gx", None, "gy"),
        P(None, "gx", None, "gy"),
        P(None, "gx", None, "gy"),
        P(("gx", "gy")),
        P(("gx", "gy"), None),
        P(("gx", "gy"), None, None),
        P(("gx", "gy")),
        P(("gx", "gy"), None),
        P(("gx", "gy"), None),
        P(("gx", "gy"), None),
    )
    out_specs = (P(None, "gx", None, "gy"), P(None, "gx", None, "gy"), P(("gx", "gy"), None))
    return jax.shard_map(
        functools.partial(per_device, mesh.shape["gx"], mesh.shape["gy"]),
        mesh=mesh,
        in_specs=in_specs,
        out_specs=out_specs,
        check_vma=False,
    )
```

profile of v0, /device:TPU:1, one launch (start us, length us, event | category | flops | bytes accessed | tf_op | source)
XLA Modules:
  0.0 54.2 jit_solution(4971710444575440702)
XLA Ops:
  0.6 0.0 copy-start.5
  0.6 0.0 copy-start.7
  0.7 0.0 copy-start.8
  0.7 0.0 copy-start.6
  0.7 0.7 %copy-done.5 = f32[256,2,4]{0,2,1:T(4,128)S(1)} copy-done((f32[256,2,4]{0,2,1:T(4,128)S(1)}, f32[256,2,4]{0,2,1:T(4,128)}, u32[]{:S(2)}) %copy-start.5) | copy-done | bytes 8216
  1.3 0.0 copy-done.7
  1.3 0.0 copy-done.8
  1.3 0.0 copy-done.6
  1.4 0.0 copy-start
  1.4 1.0 %copy-done = f32[3,4,48,128]{3,2,1,0:T(8,128)S(1)} copy-done((f32[3,4,48,128]{3,2,1,0:T(8,128)S(1)}, f32[3,4,48,128]{3,2,1,0:T(8,128)}, u32[]{:S(2)}) %copy-start) | copy-done | bytes 294936
  2.3 0.0 copy-start.1
  2.3 0.9 %copy-done.1 = f32[2,4,48,128]{3,2,1,0:T(8,128)S(1)} copy-done((f32[2,4,48,128]{3,2,1,0:T(8,128)S(1)}, f32[2,4,48,128]{3,2,1,0:T(8,128)}, u32[]{:S(2)}) %copy-start.1) | copy-done | bytes 196632
  3.3 0.0 copy-start.2
  3.3 0.9 %copy-done.2 = f32[2,4,48,128]{3,2,1,0:T(8,128)S(1)} copy-done((f32[2,4,48,128]{3,2,1,0:T(8,128)S(1)}, f32[2,4,48,128]{3,2,1,0:T(8,128)}, u32[]{:S(2)}) %copy-start.2) | copy-done | bytes 196632
  4.2 0.0 copy-start.3
  4.2 0.9 %copy-done.3 = f32[4,48,128]{2,1,0:T(8,128)S(1)} copy-done((f32[4,48,128]{2,1,0:T(8,128)S(1)}, f32[4,48,128]{2,1,0:T(8,128)}, u32[]{:S(2)}) %copy-start.3) | copy-done | bytes 98328
  5.1 0.0 copy-start.4
  5.1 0.7 %copy-done.4 = f32[32,128]{1,0:T(8,128)S(1)} copy-done((f32[32,128]{1,0:T(8,128)S(1)}, f32[32,128]{1,0:T(8,128)}, u32[]{:S(2)}) %copy-start.4) | copy-done | bytes 16408
  5.8 0.0 copy-start.9
  5.8 0.7 %copy-done.9 = s32[32]{0:T(128)S(1)} copy-done((s32[32]{0:T(128)S(1)}, s32[32]{0:T(128)}, u32[]{:S(2)}) %copy-start.9) | copy-done | bytes 152
  6.4 0.0 copy-start.10
  6.4 0.7 %copy-done.10 = s32[32,1]{0,1:T(1,128)S(1)} copy-done((s32[32,1]{0,1:T(1,128)S(1)}, s32[32,1]{0,1:T(1,128)}, u32[]{:S(2)}) %copy-start.10) | copy-done | bytes 152
  7.1 45.2 %whole.1 = (f32[2,4,48,128]{3,2,1,0:T(8,128)S(1)}, f32[2,4,48,128]{3,2,1,0:T(8,128)S(1)}, f32[2,32]{1,0:T(2,128)S(1)}) custom-call(f32[2,4,48,128]{3,2,1,0:T(8,128)S(1)} %copy-done.1, f32[4,48,128]{2,1,0:T(8,128)S(1)} %copy-done.3, f32[3,4,48,128]{3,2,1,0:T(8,128)S(1)} %copy-done, f32[2,4,48,128]{3,2,1,0:T(8,128)S(1)} %copy-done.2, s32[1,256]{1,0:T(1,128)S(1)} %bitcast.8, ...), custom_call_target="tpu_custom_call" | custom-call | tf_op jit(solution)/shard_map/whole/pallas_call | solution.py:671
  52.3 0.7 %copy.17 = f32[2,4,48,128]{3,2,1,0:T(8,128)} copy(f32[2,4,48,128]{3,2,1,0:T(8,128)S(1)} %get-tuple-element.12) | data formatting | bytes 393216
  53.0 0.7 %copy.18 = f32[2,4,48,128]{3,2,1,0:T(8,128)} copy(f32[2,4,48,128]{3,2,1,0:T(8,128)S(1)} %get-tuple-element.13) | data formatting | bytes 393216
  53.7 0.6 %copy.19 = f32[32,2]{0,1:T(2,128)} copy(f32[32,2]{0,1:T(2,128)S(1)} %bitcast.11) | data formatting | bytes 512
Async XLA Ops:
  0.6 0.7 %copy-start.5 = (f32[256,2,4]{0,2,1:T(4,128)S(1)}, f32[256,2,4]{0,2,1:T(4,128)}, u32[]{:S(2)}) copy-start(f32[256,2,4]{0,2,1:T(4,128)} %param.17) | copy-start | bytes 24580
  0.6 0.7 %copy-start.7 = (s32[256,1]{0,1:T(1,128)S(1)}, s32[256,1]{0,1:T(1,128)}, u32[]{:S(2)}) copy-start(s32[256,1]{0,1:T(1,128)} %param.16) | copy-start | bytes 3076
  0.7 0.7 %copy-start.8 = (f32[32,2]{0,1:T(2,128)S(1)}, f32[32,2]{0,1:T(2,128)}, u32[]{:S(2)}) copy-start(f32[32,2]{0,1:T(2,128)} %param.20) | copy-start | bytes 772
  0.7 0.7 %copy-start.6 = (s32[256]{0:T(256)S(1)}, s32[256]{0:T(256)}, u32[]{:S(2)}) copy-start(s32[256]{0:T(256)} %param.15) | copy-start | bytes 3076
  1.4 1.0 %copy-start = (f32[3,4,48,128]{3,2,1,0:T(8,128)S(1)}, f32[3,4,48,128]{3,2,1,0:T(8,128)}, u32[]{:S(2)}) copy-start(f32[3,4,48,128]{3,2,1,0:T(8,128)} %vel_h.1) | copy-start | bytes 884740
  2.3 0.9 %copy-start.1 = (f32[2,4,48,128]{3,2,1,0:T(8,128)S(1)}, f32[2,4,48,128]{3,2,1,0:T(8,128)}, u32[]{:S(2)}) copy-start(f32[2,4,48,128]{3,2,1,0:T(8,128)} %c0_h.1) | copy-start | bytes 589828
  3.3 0.9 %copy-start.2 = (f32[2,4,48,128]{3,2,1,0:T(8,128)S(1)}, f32[2,4,48,128]{3,2,1,0:T(8,128)}, u32[]{:S(2)}) copy-start(f32[2,4,48,128]{3,2,1,0:T(8,128)} %tgt_h.1) | copy-start | bytes 589828
  4.2 0.9 %copy-start.3 = (f32[4,48,128]{2,1,0:T(8,128)S(1)}, f32[4,48,128]{2,1,0:T(8,128)}, u32[]{:S(2)}) copy-start(f32[4,48,128]{2,1,0:T(8,128)} %kap_h.1) | copy-start | bytes 294916
  5.1 0.7 %copy-start.4 = (f32[32,128]{1,0:T(8,128)S(1)}, f32[32,128]{1,0:T(8,128)}, u32[]{:S(2)}) copy-start(f32[32,128]{1,0:T(8,128)} %foot_r.1) | copy-start | bytes 49156
  5.8 0.7 %copy-start.9 = (s32[32]{0:T(128)S(1)}, s32[32]{0:T(128)}, u32[]{:S(2)}) copy-start(s32[32]{0:T(128)} %param.18) | copy-start | bytes 388
  6.4 0.7 %copy-start.10 = (s32[32,1]{0,1:T(1,128)S(1)}, s32[32,1]{0,1:T(1,128)}, u32[]{:S(2)}) copy-start(s32[32,1]{0,1:T(1,128)} %param.19) | copy-start | bytes 388
where the time goes:
time: 54.7 us; the launch traced here: 54.2 us
  Pallas kernels  45.2 us (83%)
  local copies, waits for them, and re-layouts  8.34 us (15%)
  between operations  0.68 us (1%)
    pallas_call x1, Pallas kernels, per_device(): pl.pallas_call(functools.partial(whole_kernel, gxn, gyn), out_shape=(big,...  45.2 us
    unnamed x25, local copies, waits for them, and re-layouts  8.34 us

commit v1 on v0

--- a/solution.py
+++ b/solution.py
@@ -95,6 +95,16 @@
     kap_h,
     vel_h,
     tgt_h,
+    cell_h,
+    own_h,
+    obs_h,
+    ablk_h,
+    aown_h,
+    ctl_h,
+    foot_h,
+    out_c,
+    out_s,
+    out_g,
     cell_r,
     own_r,
     obs_r,
@@ -102,9 +112,6 @@
     aown_r,
     ctl_r,
     foot_r,
-    out_c,
-    out_s,
-    out_g,
     fields,
     kap,
     velx,
@@ -146,6 +153,22 @@
     lg_y = gyn.bit_length() - 1
     mid = slice(Z0, Z0 + NZ)
 
+    smalls = [
+        pltpu.make_async_copy(source, sink, loc_sem.at[5 + i])
+        for i, (source, sink) in enumerate(
+            (
+                (aown_h, aown_r),
+                (ablk_h, ablk_r),
+                (ctl_h, ctl_r),
+                (foot_h, foot_r),
+                (own_h, own_r),
+                (cell_h, cell_r),
+                (obs_h, obs_r),
+            )
+        )
+    ]
+    for load in smalls:
+        load.start()
     loads = [
         pltpu.make_async_copy(c0_h, fields.at[0, :, 1 : 1 + CX, mid, :], loc_sem.at[0]),
         pltpu.make_async_copy(kap_h, kap.at[1 : 1 + CX, mid, :], loc_sem.at[1]),
@@ -170,6 +193,8 @@
             barrier, inc=1, device_id=(lax.rem(me_x + t, gxn), me_y), device_id_type=MESH
         )
 
+    for load in smalls:
+        load.wait()
     rows = gyn * 8
     acts = aown_r.shape[1]
     aown = aown_r[...]
@@ -646,6 +671,19 @@
         sn2_copy(t, True).wait_send()
 
 
+def store_kernel(state, sensitivity, gradient, out_c, out_s, out_g, sem):
+    copies = [
+        pltpu.make_async_copy(source, sink, sem.at[i])
+        for i, (source, sink) in enumerate(
+            ((state, out_c), (sensitivity, out_s), (gradient, out_g))
+        )
+    ]
+    for copy in copies:
+        copy.start()
+    for copy in copies:
+        copy.wait()
+
+
 def per_device(
     gxn,
     gyn,
@@ -664,16 +702,27 @@
     sens = sensor_cell.shape[0]
     acts = actuator_block.shape[0]
     rows = gyn * 8
-    hbm = pl.BlockSpec(memory_space=pl.ANY)
+    hbm = pl.BlockSpec(memory_space=pltpu.HBM)
     vmem = pl.BlockSpec(memory_space=pltpu.VMEM)
     dma = pltpu.SemaphoreType.DMA
     big = jax.ShapeDtypeStruct((2, CX, NZ, CY), F32)
     state, sensitivity, gradient = pl.pallas_call(
         functools.partial(whole_kernel, gxn, gyn),
-        out_shape=(big, big, jax.ShapeDtypeStruct((2, acts), F32)),
-        in_specs=[hbm] * 4 + [vmem] * 7,
+        out_shape=(
+            pltpu.VMEM((2, CX, NZ, CY), F32),
+            pltpu.VMEM((2, CX, NZ, CY), F32),
+            pltpu.VMEM((2, acts), F32),
+        ),
+        in_specs=[hbm] * 11,
         out_specs=(vmem, vmem, vmem),
         scratch_shapes=[
+            pltpu.VMEM((1, sens), jnp.int32),
+            pltpu.VMEM((1, sens), jnp.int32),
+            pltpu.VMEM((2, STEPS, sens), F32),
+            pltpu.VMEM((1, acts), jnp.int32),
+            pltpu.VMEM((1, acts), jnp.int32),
+            pltpu.VMEM((2, acts), F32),
+            pltpu.VMEM((acts, CY), F32),
             pltpu.VMEM((8, 2, CX + 2, PZ, CY), F32),
             pltpu.VMEM((CX + 2, PZ, CY), F32),
             pltpu.VMEM((CX + 2, PZ, CY), F32),
@@ -696,7 +745,7 @@
             pltpu.VMEM((9, 8, CY), F32),
             pltpu.VMEM((8, CY), F32),
             pltpu.VMEM((rows, CY), F32),
-            dma((5,)),
+            dma((12,)),
             dma((10, 2)),
             dma((10, 2)),
             dma((9, 2)),
@@ -711,7 +760,7 @@
             dma((gyn,)),
         ],
         compiler_params=pltpu.CompilerParams(
-            collective_id=0, has_side_effects=True, vmem_limit_bytes=48 * 1024 * 1024
+            collective_id=0, has_side_effects=True, vmem_limit_bytes=64000000
         ),
         name="whole",
     )(
@@ -727,6 +776,15 @@
         controls.T,
         footprint,
     )
+    state, sensitivity, gradient = pl.pallas_call(
+        store_kernel,
+        out_shape=(big, big, jax.ShapeDtypeStruct((2, acts), F32)),
+        in_specs=[vmem] * 3,
+        out_specs=(hbm,) * 3,
+        scratch_shapes=[dma((3,))],
+        compiler_params=pltpu.CompilerParams(vmem_limit_bytes=1 << 20),
+        name="store",
+    )(state, sensitivity, gradient)
     return state, sensitivity, gradient.T
 
 

time: 54.7 us -> 46.7 us (0.85)
  local copies, waits for them, and re-layouts: 8.34 us -> 0 us
  Pallas kernels: 45.2 us -> 45.8 us
    unnamed x25 -> x0, local copies, waits for them, and re-layouts: 8.34 us -> none
    pallas_call x1 -> x2, Pallas kernels: 45.2 us -> 45.8 us  [the longest x1 45 us: per_device(): pl.pallas_call(functools.partial(whole_kernel, gxn, gyn), out_shape=(pltp...]
where the time goes in v1:
time: 46.7 us; the launch traced here: 46.4 us
  Pallas kernels  45.8 us (98%)
  between operations  0.64 us (1%)
    pallas_call x1, Pallas kernels, per_device(): pl.pallas_call(functools.partial(whole_kernel, gxn, gyn), out_shape=(pltp...  45 us

profile of v1, /device:TPU:1, one launch (start us, length us, event | category | flops | bytes accessed | tf_op | source)
XLA Modules:
  0.0 46.4 jit_solution(13773246678813266700)
XLA Ops:
  0.6 45.0 %whole.1 = (f32[2,4,48,128]{3,2,1,0:T(8,128)S(1)}, f32[2,4,48,128]{3,2,1,0:T(8,128)S(1)}, f32[2,32]{1,0:T(2,128)S(1)}) custom-call(f32[2,4,48,128]{3,2,1,0:T(8,128)} %c0_h.1, f32[4,48,128]{2,1,0:T(8,128)} %kap_h.1, f32[3,4,48,128]{3,2,1,0:T(8,128)} %vel_h.1, f32[2,4,48,128]{3,2,1,0:T(8,128)} %tgt_h.1, s32[1,256]{1,0:T(1,128)} %bitcast.8, s32[1,256]{1,0:T(1,128)} %bitcast.9, ...), custom_call_target="tpu_custom_call" | custom-call | tf_op jit(solution)/shard_map/whole/pallas_call | solution.py:709
  45.6 0.8 %store.1 = (f32[2,4,48,128]{3,2,1,0:T(8,128)}, f32[2,4,48,128]{3,2,1,0:T(8,128)}, f32[2,32]{1,0:T(2,128)}) custom-call(f32[2,4,48,128]{3,2,1,0:T(8,128)S(1)} %get-tuple-element.9.state, f32[2,4,48,128]{3,2,1,0:T(8,128)S(1)} %get-tuple-element.10.sensitivity, f32[2,32]{1,0:T(2,128)S(1)} %get-tuple-element.11.gradient), custom_call_target="tpu_custom_call" | custom-call | tf_op jit(solution)/shard_map/store/pallas_call | solution.py:779

commit v2 on v1

--- a/solution.py
+++ b/solution.py
@@ -63,15 +63,20 @@
     packed = jnp.zeros((8, CY), F32)
     for zv in range(ZV):
         for p, plane in enumerate(planes):
+            if plane is None:
+                continue
             q = zv * len(planes) + p
             turned = pltpu.roll(plane[zv * 8 : zv * 8 + 8], 2 * q + 1, 1)
             packed = jnp.where(lax.shift_right_logical(lane, 1) == q, turned, packed)
     return packed
 
 
-def unpack_edges(left, right, number):
+def merge_edges(left, right):
     lane = iota((8, CY), 1)
-    both = jnp.where((lane & 1) == 0, pltpu.roll(right, CY - 1, 1), pltpu.roll(left, 1, 1))
+    return jnp.where((lane & 1) == 0, pltpu.roll(right, CY - 1, 1), pltpu.roll(left, 1, 1))
+
+
+def unpack_edges(both, number):
     planes = []
     for p in range(number):
         parts = [
@@ -117,8 +122,10 @@
     velx,
     velyz,
     tgt,
-    cof_f,
-    cof_a,
+    cof,
+    pcy,
+    pcx,
+    bas,
     src,
     cnt,
     obsf,
@@ -132,6 +139,8 @@
     edge_o,
     edge_l,
     edge_r,
+    edge_d,
+    edge_u,
     grad_o,
     grad_i,
     loc_sem,
@@ -139,6 +148,8 @@
     xr_sem,
     es_sem,
     er_sem,
+    fs_sem,
+    fr_sem,
     as_sem,
     ar_sem,
     ss_sem,
@@ -254,10 +265,12 @@
     @pl.when(me_x == 0)
     def _():
         zero_side(0)
+        edge_d[...] = jnp.zeros_like(edge_d)
 
     @pl.when(me_x == gxn - 1)
     def _():
         zero_side(CX + 1)
+        edge_u[...] = jnp.zeros_like(edge_u)
 
     @pl.when(me_y == 0)
     def _():
@@ -326,6 +339,18 @@
             send_sem=es_sem.at[slot, side],
             recv_sem=er_sem.at[slot, side],
             device_id=(me_x, there),
+            device_id_type=MESH,
+        )
+
+    def edge_x_copy(slot, side):
+        there = me_x - 1 if side == 0 else me_x + 1
+        sink = edge_u if side == 0 else edge_d
+        return pltpu.make_async_remote_copy(
+            src_ref=edge_o.at[slot],
+            dst_ref=sink.at[slot],
+            send_sem=fs_sem.at[slot, side],
+            recv_sem=fr_sem.at[slot, side],
+            device_id=(there, me_y),
             device_id_type=MESH,
         )
 
@@ -373,21 +398,13 @@
     def wait_send(copy):
         copy.wait_send()
 
-    def wait_recv_x(slots):
+    def wait_recv(maker, axis, slots):
         for side in (0, 1):
 
-            @pl.when(has[0][1 - side])
+            @pl.when(has[axis][1 - side])
             def _(side=side):
                 for slot in slots:
-                    x_copy(slot, side).wait_recv()
-
-    def wait_recv_e(slots):
-        for side in (0, 1):
-
-            @pl.when(has[1][1 - side])
-            def _(side=side):
-                for slot in slots:
-                    edge_copy(slot, side).wait_recv()
+                    maker(slot, side).wait_recv()
 
     @pl.loop(1, gyn)
     def _(t):
@@ -404,9 +421,12 @@
     act_i[own_tile, :] = act_o[own_tile, :]
     sen_i[own_tile, :] = sen_o[own_tile, :]
 
-    wait_recv_x((8, 9))
-    wait_recv_e((8,))
-    halos = unpack_edges(edge_l[8], edge_r[8], 2 * CX)
+    wait_recv(x_copy, 0, (8, 9))
+    wait_recv(edge_copy, 1, (8,))
+    halos = unpack_edges(merge_edges(edge_l[8], edge_r[8]), 2 * CX)
+    lane = iota((NZ, CY), 1)
+    rim_y = [[None] * (2 * CX) for _ in range(2)]
+    rim_x = [[None] * (2 * CX) for _ in range(2)]
     for x in range(CX):
         here = kap[1 + x, mid, :]
         kyp, kym = beside_y(here, halos[x])
@@ -424,92 +444,172 @@
         uyp, uym = beside_y(uy, halos[CX + x])
         ux = velx[1 + x, mid, :]
         uz = velyz[1, x, mid, :]
-        drift_f = (-0.5 * ux, 0.5 * ux, -0.5 * uy, 0.5 * uy, -0.5 * uz, 0.5 * uz)
-        drift_a = (
-            0.5 * velx[2 + x, mid, :],
-            -0.5 * velx[x, mid, :],
-            0.5 * uyp,
-            -0.5 * uym,
-            0.5 * velyz[1, x, Z0 + 1 : Z0 + NZ + 1, :],
-            -0.5 * velyz[1, x, Z0 - 1 : Z0 + NZ - 1, :],
+        drifts = (
+            (-0.5 * ux, 0.5 * ux, -0.5 * uy, 0.5 * uy, -0.5 * uz, 0.5 * uz),
+            (
+                0.5 * velx[2 + x, mid, :],
+                -0.5 * velx[x, mid, :],
+                0.5 * uyp,
+                -0.5 * uym,
+                0.5 * velyz[1, x, Z0 + 1 : Z0 + NZ + 1, :],
+                -0.5 * velyz[1, x, Z0 - 1 : Z0 + NZ - 1, :],
+            ),
         )
         for s in range(2):
             scale = SCALES[s]
-            cof_f[s, 6, x] = 1.0 - scale * total
-            for f in range(6):
-                scaled = faces[f] if s == 0 else scale * faces[f]
-                cof_f[s, f, x] = scaled + drift_f[f]
-                cof_a[s, f, x] = scaled + drift_a[f]
-
-    def stencil(slot, cof, s, x, halo):
+            cof[0, s, 7, x] = 1.0 - scale * total
+            for d in range(2):
+                parts = []
+                for f in range(6):
+                    scaled = faces[f] if s == 0 else scale * faces[f]
+                    parts.append(scaled + drifts[d][f])
+                for f in (0, 1, 4, 5):
+                    cof[d, s, f, x] = parts[f]
+                cof[d, s, 2, x] = jnp.where(lane == CY - 1, 0.0, parts[2])
+                cof[d, s, 3, x] = jnp.where(lane == 0, 0.0, parts[3])
+                rim = jnp.where(lane == CY - 1, parts[2], jnp.where(lane == 0, parts[3], 0.0))
+                cof[d, s, 6, x] = rim
+                rim_y[d][s * CX + x] = rim
+                if x == 0:
+                    rim_x[d][s * CX + x] = parts[1]
+                if x == CX - 1:
+                    rim_x[d][s * CX + x] = parts[0]
+    for d in range(2):
+        pcy[d] = pack_edges(rim_y[d])
+        pcx[d] = pack_edges(rim_x[d])
+
+    cells = [(s, x) for x in (0, CX - 1, 1, 2) for s in range(2)]
+    x_lane = lax.shift_right_logical(iota((8, CY), 1), 1) & (CX - 1)
+
+    def base(slot, d, s, x):
         here = fields[slot, s, 1 + x, mid, :]
-        yp, ym = beside_y(here, halo)
-        return (
-            cof_f[s, 6, x] * here
-            + cof[s, 0, x] * fields[slot, s, 2 + x, mid, :]
-            + cof[s, 1, x] * fields[slot, s, x, mid, :]
-            + cof[s, 2, x] * yp
-            + cof[s, 3, x] * ym
-            + cof[s, 4, x] * fields[slot, s, 1 + x, Z0 + 1 : Z0 + NZ + 1, :]
-            + cof[s, 5, x] * fields[slot, s, 1 + x, Z0 - 1 : Z0 + NZ - 1, :]
-        )
-
-    def send_field(slot):
-        planes = [fields[slot, s, 1 + x, mid, :] for s in range(2) for x in range(CX)]
-        edge_o[slot] = pack_edges(planes)
+        value = (
+            cof[0, s, 7, x] * here
+            + cof[d, s, 2, x] * pltpu.roll(here, CY - 1, 1)
+            + cof[d, s, 3, x] * pltpu.roll(here, 1, 1)
+            + cof[d, s, 4, x] * fields[slot, s, 1 + x, Z0 + 1 : Z0 + NZ + 1, :]
+            + cof[d, s, 5, x] * fields[slot, s, 1 + x, Z0 - 1 : Z0 + NZ - 1, :]
+        )
+        if x < CX - 1:
+            value = value + cof[d, s, 0, x] * fields[slot, s, 2 + x, mid, :]
+        if x > 0:
+            value = value + cof[d, s, 1, x] * fields[slot, s, x, mid, :]
+        return value
+
+    def base_all(slot, d, extra):
+        planes = [None] * (2 * CX)
+        for s, x in cells:
+            value = base(slot, d, s, x)
+            if extra is not None:
+                value = value + extra(s, x)
+            bas[s, x] = value
+            planes[s * CX + x] = value
+        return planes
+
+    def finish(slot, d, s, x, halo):
+        value = bas[s, x] + cof[d, s, 6, x] * halo
+        if x == 0:
+            value = value + cof[d, s, 1, x] * fields[slot, s, 0, mid, :]
+        if x == CX - 1:
+            value = value + cof[d, s, 0, x] * fields[slot, s, CX + 1, mid, :]
+        return value
+
+    def take_y(slot):
+        wait_recv(edge_copy, 1, (slot,))
+        return merge_edges(edge_l[slot], edge_r[slot])
+
+    def next_edges(slot, d, rim, packed):
+        wait_recv(edge_x_copy, 0, (slot,))
+        across = jnp.where(
+            x_lane == 0, pltpu.roll(edge_d[slot], CY - 6, 1), pltpu.roll(edge_u[slot], 6, 1)
+        )
+        return packed + pcy[d] * rim + pcx[d] * across
+
+    def send_edges(slot, value):
+        edge_o[slot] = value
         both_sides(edge_copy, 1, start, (slot,))
-        both_sides(x_copy, 0, start, (slot,))
-
-    def take_field(slot):
-        wait_recv_x((slot,))
-        wait_recv_e((slot,))
-        return unpack_edges(edge_l[slot], edge_r[slot], 2 * CX)
-
-    halos = take_field(0)
-    for s in range(2):
-        for x in range(CX):
-            fields[1, s, 1 + x, mid, :] = stencil(0, cof_f, s, x, halos[s * CX + x])
+        if slot < 7:
+            both_sides(edge_x_copy, 0, start, (slot,))
+
+    def put_field(slot, s, x, value):
+        fields[slot, s, 1 + x, mid, :] = value
+        if x == CX - 1 and s == 1:
+            both_sides(x_copy, 0, start, (slot,))
+
+    base_all(0, 0, None)
+    rim = take_y(0)
+    wait_recv(x_copy, 0, (0,))
+    halos = unpack_edges(rim, 2 * CX)
+    for s, x in cells:
+        bas[s, x] = finish(0, 0, s, x, halos[s * CX + x])
 
     @pl.loop(1, gyn)
     def _(t):
         act_of(t).wait_recv()
 
-    got = act_i[...]
-    moved = pltpu.roll(got, rows - 4, 0)
-    sel = (iota((8, CY), 0) == iota((8, CY), 1)).astype(F32)
-    metas = dot_nt(sel, moved, HIGH)
-    blk_row = (metas[0:1] + 0.5).astype(jnp.int32) - 1
-    live_row = ((iota((1, rows), 1) & 7) < 4) & (blk_row >= 0)
-    bz_row = jnp.where(live_row, lax.shift_right_arithmetic(blk_row, 5), -1)
-    blk_col = (moved[:, 0:1] + 0.5).astype(jnp.int32) - 1
-    live_col = ((iota((rows, 1), 0) & 7) < 4) & (blk_col >= 0)
-    first_y = jnp.where(live_col, (blk_col & 31) * FY, -8)
-    at_y = [(iota((rows, CY), 1) == first_y + fy).astype(F32) for fy in range(FY)]
+    many_a = gyn * 4
+    sub = iota((8, CY), 0)
+    foots, metas = [], []
+    for i in range(gyn // 2):
+        one, two = act_i[16 * i : 16 * i + 8, :], act_i[16 * i + 8 : 16 * i + 16, :]
+        foots.append(jnp.where(sub < 4, one, pltpu.roll(two, 4, 0)))
+        metas.append(jnp.where(sub < 4, pltpu.roll(one, 4, 0), two))
+    foot = jnp.concatenate(foots * 2, axis=0)
+    meta = jnp.concatenate(metas * 2, axis=0)
+    sel = (iota((8, CY), 0) == iota((8, CY), 1)).astype(BF16)
+    meta_parts = split3(meta)
+    m0, m1, m2 = [dot_nt(sel, part) for part in meta_parts]
+    meta_rows = m0 + m1 + m2
+    blk_row = (meta_rows[0:1] + 0.5).astype(jnp.int32) - 1
+    bz_row = jnp.where(blk_row >= 0, lax.shift_right_arithmetic(blk_row, 5), -1)
+    blk_col = (meta[:, 0:1] + 0.5).astype(jnp.int32) - 1
+    half_col = (iota((2 * many_a, 1), 0) >= many_a).astype(jnp.int32)
+    first_y = jnp.where(blk_col >= 0, (blk_col & 31) * FY + half_col, -8)
+    at_y = [
+        (iota((2 * many_a, CY), 1) == first_y + 2 * g).astype(F32).astype(BF16)
+        for g in range(2)
+    ]
     perm_row = iota((CY, CY), 0)
     perm = (
-        iota((CY, CY), 1) == (perm_row & 31) * FY + lax.shift_right_logical(perm_row, 5)
-    ).astype(F32)
-    foot_t = dot_nt(perm, got, HIGH)
+        (iota((CY, CY), 1) == (perm_row & 31) * FY + lax.shift_right_logical(perm_row, 5))
+        .astype(F32)
+        .astype(BF16)
+    )
+    f0, f1, f2 = [dot_nt(perm, part) for part in split3(foot)]
+    foot_t = f0 + f1 + f2
+    half_row = iota((32, 2 * many_a), 1) < many_a
+    foot_g = [
+        jnp.where(half_row, foot_t[64 * g : 64 * g + 32], foot_t[64 * g + 32 : 64 * g + 64])
+        for g in range(2)
+    ]
     weights = [
-        jnp.where(bz_row == bz, metas[1 + s : 2 + s], 0.0)
+        jnp.where(bz_row == bz, meta_rows[1 + s : 2 + s], 0.0)
         for s in range(2)
         for bz in range(BZ)
     ]
-    placed = jnp.zeros((2 * BZ * 32, CY), F32)
-    for fy in range(FY):
-        part = foot_t[fy * 32 : fy * 32 + 32]
-        left = jnp.concatenate([part * w for w in weights], axis=0)
-        placed = placed + dot_nn(left, at_y[fy], HIGH)
+    spots = jnp.concatenate(at_y, axis=0)
     for s in range(2):
+        left = jnp.concatenate(
+            [
+                jnp.concatenate([foot_g[g] * weights[s * BZ + bz] for bz in range(BZ)], axis=0)
+                for g in range(2)
+            ],
+            axis=1,
+        )
+        p0, p1, p2 = [dot_nn(part, spots) for part in split3(left)]
+        placed = p0 + p1 + p2
         for bz in range(BZ):
             for fx in range(FX):
-                row = (s * BZ + bz) * 32 + fx * 8
+                row = bz * 32 + fx * 8
                 src[s, fx, bz * 8 : bz * 8 + 8, :] = placed[row : row + 8]
 
-    for s in range(2):
-        for x in range(CX):
-            fields[1, s, 1 + x, mid, :] = fields[1, s, 1 + x, mid, :] + src[s, x]
-    send_field(1)
+    planes = [None] * (2 * CX)
+    for s, x in cells:
+        value = bas[s, x] + src[s, x]
+        planes[s * CX + x] = value
+        fields[1, s, 1 + x, mid, :] = value
+    send_edges(1, pack_edges(planes))
+    both_sides(x_copy, 0, start, (1,))
 
     @pl.loop(1, gyn)
     def _(t):
@@ -535,20 +635,16 @@
 
     sn2_i[me_x] = sn2_o[me_x]
 
-    def step_forward(slot, sink):
-        halos = take_field(slot)
-        for s in range(2):
-            for x in range(CX):
-                sink(s, x, stencil(slot, cof_f, s, x, halos[s * CX + x]) + src[s, x])
-
-    def into(slot):
-        def put(s, x, value):
-            fields[slot, s, 1 + x, mid, :] = value
-
-        return put
-
-    step_forward(1, into(2))
-    send_field(2)
+    supply = lambda s, x: src[s, x]
+    packed = pack_edges(base_all(1, 0, supply))
+
+    rim = take_y(1)
+    send_edges(2, next_edges(1, 0, rim, packed))
+    wait_recv(x_copy, 0, (1,))
+    halos = unpack_edges(rim, 2 * CX)
+    for s, x in cells:
+        put_field(2, s, x, finish(1, 0, s, x, halos[s * CX + x]))
+    packed = pack_edges(base_all(2, 0, supply))
 
     @pl.loop(1, gxn)
     def _(t):
@@ -556,60 +652,84 @@
 
     records = jnp.concatenate([sn2_i[d] for d in range(gxn)], axis=0)
     many = records.shape[0]
-    sel = (iota((8, CY), 0) * 16 == iota((8, CY), 1)).astype(F32)
-    cell_rows = (dot_nt(sel, records, HIGH) + 0.5).astype(jnp.int32) - 1
-    zx = lax.shift_right_arithmetic(cell_rows, 7)
-    pick_zx = jnp.concatenate(
-        [(iota((CX * NZ, many), 0) == zx[k : k + 1]).astype(BF16) for k in range(4)], axis=1
-    )
-    at_lane = []
+    take = (iota((64, CY), 0) == iota((64, CY), 1)).astype(BF16)
+    r0, r1, r2 = [dot_nt(take, part) for part in split3(records)]
+    lanes_t = r0 + r1 + r2
+    pick_zx, at_lane = [], []
     for k in range(4):
+        cell_row = (lanes_t[16 * k : 16 * k + 1] + 0.5).astype(jnp.int32) - 1
+        zx = lax.shift_right_arithmetic(cell_row, 7)
+        pick_zx.append(iota((CX * NZ, many), 0) == zx)
         cell_col = (records[:, 16 * k : 16 * k + 1] + 0.5).astype(jnp.int32) - 1
-        lane = jnp.where(cell_col >= 0, cell_col & (CY - 1), -1)
-        at_lane.append(iota((many, CY), 1) == lane)
-    cnt[...] = dot_nn(
-        pick_zx, jnp.concatenate([a.astype(F32).astype(BF16) for a in at_lane], axis=0)
-    )
-    for ch in range(2 * STEPS):
-        values = jnp.concatenate(
-            [
-                jnp.where(at_lane[k], records[:, 16 * k + 1 + ch : 16 * k + 2 + ch], 0.0)
-                for k in range(4)
-            ],
-            axis=0,
-        )
-        hi, mid_part, low = split3(values)
-        obsf[ch] = (dot_nn(pick_zx, hi) + dot_nn(pick_zx, mid_part)) + dot_nn(pick_zx, low)
-
-    step_forward(2, into(3))
-    send_field(3)
+        where_y = jnp.where(cell_col >= 0, cell_col & (CY - 1), -1)
+        at_lane.append((iota((many, CY), 1) == where_y).astype(F32).astype(BF16))
+    at_lanes = jnp.concatenate(at_lane, axis=0)
+    one_zx = jnp.concatenate([p.astype(F32).astype(BF16) for p in pick_zx], axis=1)
+    cnt[...] = dot_nn(one_zx, at_lanes)
+
+    def sensor_field(ch):
+        rows_of = [lanes_t[16 * k + 1 + ch : 16 * k + 2 + ch] for k in range(4)]
+        left = jnp.concatenate(
+            [jnp.where(pick_zx[k], rows_of[k], 0.0) for k in range(4)], axis=1
+        )
+        o0, o1, o2 = [dot_nn(part, at_lanes) for part in split3(left)]
+        obsf[ch] = o0 + o1 + o2
+
+    for s in range(2):
+        for n in (4, 3):
+            sensor_field(s * STEPS + n - 1)
+
+    rim = take_y(2)
+    send_edges(3, next_edges(2, 0, rim, packed))
+    wait_recv(x_copy, 0, (2,))
+    halos = unpack_edges(rim, 2 * CX)
+    for s, x in cells:
+        put_field(3, s, x, finish(2, 0, s, x, halos[s * CX + x]))
+    packed = pack_edges(base_all(3, 0, supply))
+
+    for s in range(2):
+        for n in (2, 1):
+            sensor_field(s * STEPS + n - 1)
+
+    def span(x):
+        return slice(x * NZ, x * NZ + NZ)
 
     def forcing(state, s, x, n):
-        span = slice(x * NZ, x * NZ + NZ)
-        return cnt[span] * state - obsf[s * STEPS + n - 1, span]
+        return cnt[span(x)] * state - obsf[s * STEPS + n - 1, span(x)]
 
     loads[4].wait()
-
-    def last(s, x, value):
+    packed_cnt = pack_edges([cnt[span(x)] for s in range(2) for x in range(CX)])
+    packed_goal = pack_edges(
+        [tgt[s, x] + obsf[s * STEPS + 3, span(x)] for s in range(2) for x in range(CX)]
+    )
+
+    rim = take_y(3)
+    edges = next_edges(3, 0, rim, packed)
+    send_edges(4, edges + packed_cnt * edges - packed_goal)
+    wait_recv(x_copy, 0, (3,))
+    halos = unpack_edges(rim, 2 * CX)
+    for s, x in cells:
+        value = finish(3, 0, s, x, halos[s * CX + x])
         out_c[s, x] = value
         adj = value - tgt[s, x] + forcing(value, s, x, 4)
-        fields[4, s, 1 + x, mid, :] = adj
         summed[s, x] = adj
-
-    step_forward(3, last)
-    send_field(4)
+        put_field(4, s, x, adj)
 
     for n in (3, 2, 1):
         slot = 7 - n
-        halos = take_field(slot)
-        for s in range(2):
-            for x in range(CX):
-                adj = stencil(slot, cof_a, s, x, halos[s * CX + x]) + forcing(
-                    fields[n, s, 1 + x, mid, :], s, x, n
-                )
-                fields[slot + 1, s, 1 + x, mid, :] = adj
-                summed[s, x] = summed[s, x] + adj
-        send_field(slot + 1)
+        packed = pack_edges(
+            base_all(
+                slot, 1, lambda s, x: forcing(fields[n, s, 1 + x, mid, :], s, x, n)
+            )
+        )
+        rim = take_y(slot)
+        send_edges(slot + 1, next_edges(slot, 1, rim, packed))
+        wait_recv(x_copy, 0, (slot,))
+        halos = unpack_edges(rim, 2 * CX)
+        for s, x in cells:
+            adj = finish(slot, 1, s, x, halos[s * CX + x])
+            summed[s, x] = summed[s, x] + adj
+            put_field(slot + 1, s, x, adj)
 
     stacked = jnp.concatenate(
         [
@@ -620,18 +740,23 @@
         ],
         axis=0,
     )
-    totals = [jnp.zeros((32, rows), F32) for _ in range(2)]
-    picked = [dot_nt(stacked, at_y[fy], HIGH) for fy in range(FY)]
+    sums = []
     for s in range(2):
-        for bz in range(BZ):
-            base = (s * BZ + bz) * 32
-            part = jnp.zeros((32, rows), F32)
-            for fy in range(FY):
-                part = part + foot_t[fy * 32 : fy * 32 + 32] * picked[fy][base : base + 32]
-            totals[s] = totals[s] + jnp.where(bz_row == bz, part, 0.0)
-    sums = [jnp.sum(t, axis=0, keepdims=True) for t in totals]
-    if rows < CY:
-        sums = [jnp.concatenate([v, jnp.zeros((1, CY - rows), F32)], axis=1) for v in sums]
+        parts = split3(stacked[s * BZ * 32 : (s + 1) * BZ * 32])
+        total = jnp.zeros((32, 2 * many_a), F32)
+        for g in range(2):
+            q0, q1, q2 = [dot_nt(part, at_y[g]) for part in parts]
+            picked = q0 + q1 + q2
+            part = jnp.zeros((32, 2 * many_a), F32)
+            for bz in range(BZ):
+                part = part + jnp.where(bz_row == bz, picked[bz * 32 : bz * 32 + 32], 0.0)
+            total = total + foot_g[g] * part
+        both = jnp.sum(total, axis=0, keepdims=True)
+        sums.append(both + pltpu.roll(both, many_a, 1))
+    if 2 * many_a < CY:
+        sums = [
+            jnp.concatenate([v, jnp.zeros((1, CY - 2 * many_a), F32)], axis=1) for v in sums
+        ]
     grad_o[...] = jnp.concatenate(sums + [jnp.zeros((6, CY), F32)], axis=0)
 
     @pl.loop(1, gyn)
@@ -640,16 +765,18 @@
 
     grad_i[own_tile, :] = grad_o[...]
 
-    halos = take_field(7)
-    for s in range(2):
-        for x in range(CX):
-            out_s[s, x] = stencil(7, cof_a, s, x, halos[s * CX + x])
+    base_all(7, 1, None)
+    rim = take_y(7)
+    wait_recv(x_copy, 0, (7,))
+    halos = unpack_edges(rim, 2 * CX)
+    for s, x in cells:
+        out_s[s, x] = finish(7, 1, s, x, halos[s * CX + x])
 
     @pl.loop(1, gyn)
     def _(t):
         grad_of(t).wait_recv()
 
-    pick_lane = (iota((CY, acts), 0) == me_y * 8 + arank).astype(F32)
+    pick_lane = (iota((CY, acts), 0) == me_y * 4 + arank).astype(F32)
     brought = dot_nn(grad_i[...], pick_lane, HIGH)
     mine = jnp.where(to_tile, brought, 0.0)
     for s in range(2):
@@ -659,6 +786,7 @@
 
     both_sides(edge_copy, 1, wait_send, range(9))
     both_sides(x_copy, 0, wait_send, range(10))
+    both_sides(edge_x_copy, 0, wait_send, range(1, 7))
 
     @pl.loop(1, gyn)
     def _(t):
@@ -728,8 +856,10 @@
             pltpu.VMEM((CX + 2, PZ, CY), F32),
             pltpu.VMEM((2, CX, PZ, CY), F32),
             pltpu.VMEM((2, CX, NZ, CY), F32),
-            pltpu.VMEM((2, 7, CX, NZ, CY), F32),
-            pltpu.VMEM((2, 6, CX, NZ, CY), F32),
+            pltpu.VMEM((2, 2, 8, CX, NZ, CY), F32),
+            pltpu.VMEM((2, 8, CY), F32),
+            pltpu.VMEM((2, 8, CY), F32),
+            pltpu.VMEM((2, CX, NZ, CY), F32),
             pltpu.VMEM((2, CX, NZ, CY), F32),
             pltpu.VMEM((CX * NZ, CY), F32),
             pltpu.VMEM((2 * STEPS, CX * NZ, CY), F32),
@@ -743,6 +873,8 @@
             pltpu.VMEM((9, 8, CY), F32),
             pltpu.VMEM((9, 8, CY), F32),
             pltpu.VMEM((9, 8, CY), F32),
+            pltpu.VMEM((7, 8, CY), F32),
+            pltpu.VMEM((7, 8, CY), F32),
             pltpu.VMEM((8, CY), F32),
             pltpu.VMEM((rows, CY), F32),
             dma((12,)),
@@ -750,6 +882,8 @@
             dma((10, 2)),
             dma((9, 2)),
             dma((9, 2)),
+            dma((7, 2)),
+            dma((7, 2)),
             dma((gyn,)),
             dma((gyn,)),
             dma((gyn,)),

time: 46.7 us -> 44.6 us (0.955)
  Pallas kernels: 45.8 us -> 43.6 us
    pallas_call x1, Pallas kernels: 45 us -> 42.9 us  [per_device(): pl.pallas_call(functools.partial(whole_kernel, gxn, gyn), out_shape=(pltp...]
where the time goes in v2:
time: 44.6 us; the launch traced here: 44.3 us
  Pallas kernels  43.6 us (98%)
  between operations  0.64 us (1%)
    pallas_call x1, Pallas kernels, per_device(): pl.pallas_call(functools.partial(whole_kernel, gxn, gyn), out_shape=(pltp...  42.9 us

profile of v2, /device:TPU:1, one launch (start us, length us, event | category | flops | bytes accessed | tf_op | source)
XLA Modules:
  0.0 44.3 jit_solution(14132038808232773190)
XLA Ops:
  0.6 42.9 %whole.1 = (f32[2,4,48,128]{3,2,1,0:T(8,128)S(1)}, f32[2,4,48,128]{3,2,1,0:T(8,128)S(1)}, f32[2,32]{1,0:T(2,128)S(1)}) custom-call(f32[2,4,48,128]{3,2,1,0:T(8,128)} %c0_h.1, f32[4,48,128]{2,1,0:T(8,128)} %kap_h.1, f32[3,4,48,128]{3,2,1,0:T(8,128)} %vel_h.1, f32[2,4,48,128]{3,2,1,0:T(8,128)} %tgt_h.1, s32[1,256]{1,0:T(1,128)} %bitcast.8, s32[1,256]{1,0:T(1,128)} %bitcast.9, ...), custom_call_target="tpu_custom_call" | custom-call | tf_op jit(solution)/shard_map/whole/pallas_call | solution.py:837
  43.5 0.8 %store.1 = (f32[2,4,48,128]{3,2,1,0:T(8,128)}, f32[2,4,48,128]{3,2,1,0:T(8,128)}, f32[2,32]{1,0:T(2,128)}) custom-call(f32[2,4,48,128]{3,2,1,0:T(8,128)S(1)} %get-tuple-element.9.state, f32[2,4,48,128]{3,2,1,0:T(8,128)S(1)} %get-tuple-element.10.sensitivity, f32[2,32]{1,0:T(2,128)S(1)} %get-tuple-element.11.gradient), custom_call_target="tpu_custom_call" | custom-call | tf_op jit(solution)/shard_map/store/pallas_call | solution.py:913

commit v3 on v2

--- a/solution.py
+++ b/solution.py
@@ -58,32 +58,70 @@
     return jnp.sum(onehot * before, axis=0, keepdims=True).astype(jnp.int32)
 
 
-def pack_edges(planes):
-    lane = iota((8, CY), 1)
-    packed = jnp.zeros((8, CY), F32)
-    for zv in range(ZV):
-        for p, plane in enumerate(planes):
-            if plane is None:
-                continue
-            q = zv * len(planes) + p
-            turned = pltpu.roll(plane[zv * 8 : zv * 8 + 8], 2 * q + 1, 1)
-            packed = jnp.where(lax.shift_right_logical(lane, 1) == q, turned, packed)
-    return packed
-
-
-def merge_edges(left, right):
-    lane = iota((8, CY), 1)
-    return jnp.where((lane & 1) == 0, pltpu.roll(right, CY - 1, 1), pltpu.roll(left, 1, 1))
-
-
-def unpack_edges(both, number):
-    planes = []
-    for p in range(number):
-        parts = [
-            pltpu.roll(both, CY - (2 * (zv * number + p) + 1), 1) for zv in range(ZV)
-        ]
-        planes.append(jnp.concatenate(parts, axis=0))
-    return planes
+def lanes8():
+    return iota((8, CY), 1)
+
+
+def pack_cols(planes):
+    group = lax.shift_right_logical(lanes8(), 3)
+    tiles = []
+    for j in range(ZV // 2):
+        tile = jnp.zeros((8, CY), F32)
+        for odd in range(2):
+            zv = 2 * j + odd
+            for p, plane in enumerate(planes):
+                turned = pltpu.roll(plane[zv * 8 : zv * 8 + 8], 8 * p + 4 + 64 * odd, 1)
+                tile = jnp.where(group == p + 8 * odd, turned, tile)
+        tiles.append(tile)
+    return jnp.concatenate(tiles, axis=0)
+
+
+def join_cols(own, left, right):
+    lane = lanes8()
+    low, first = lane < 64, (lane & 7) < 4
+    rows = []
+    for j in range(ZV // 2):
+        part = slice(8 * j, 8 * j + 8)
+        lhs = jnp.where(first, left[part], own[part])
+        rhs = jnp.where(first, own[part], right[part])
+        rows.append(jnp.where(low, lhs, pltpu.roll(rhs, 64, 1)))
+        rows.append(jnp.where(low, pltpu.roll(lhs, 64, 1), rhs))
+    return jnp.concatenate(rows, axis=0)
+
+
+def halo_planes(region, number):
+    lane = iota((NZ, CY), 1)
+    both = jnp.where((lane & 7) == 4, pltpu.roll(region, 1, 1), pltpu.roll(region, 63, 1))
+    return [pltpu.roll(both, CY - (8 * p + 4), 1) for p in range(number)]
+
+
+def squeeze_x(region, x):
+    slot = lax.shift_right_logical(lanes8(), 3) & 3
+    tiles = []
+    for first in (0, 4):
+        tile = jnp.zeros((8, CY), F32)
+        for k in range(first, min(first + 4, ZV)):
+            shift = (8 * (k - first - x)) % CY
+            part = region[8 * k : 8 * k + 8]
+            tile = jnp.where(slot == k - first, pltpu.roll(part, shift, 1) if shift else part, tile)
+        tiles.append(tile)
+    return jnp.concatenate(tiles, axis=0)
+
+
+def spread_x(tiles, x):
+    rows = []
+    for k in range(ZV):
+        shift = (8 * (x - k % 4)) % CY
+        part = tiles[8 * (k // 4) : 8 * (k // 4) + 8]
+        rows.append(pltpu.roll(part, shift, 1) if shift else part)
+    return jnp.concatenate(rows, axis=0)
+
+
+def beside_x(region, below, above):
+    slot = lax.shift_right_logical(iota((NZ, CY), 1), 3) & 3
+    minus = jnp.where(slot == 0, spread_x(below, 0), pltpu.roll(region, 8, 1))
+    plus = jnp.where(slot == 3, spread_x(above, 3), pltpu.roll(region, CY - 8, 1))
+    return plus, minus
 
 
 def beside_y(plane, halo):
@@ -123,8 +161,9 @@
     velyz,
     tgt,
     cof,
-    pcy,
-    pcx,
+    rim_f,
+    rim_c,
+    rim_k,
     bas,
     src,
     cnt,
@@ -139,8 +178,9 @@
     edge_o,
     edge_l,
     edge_r,
-    edge_d,
-    edge_u,
+    rim_o,
+    rim_d,
+    rim_u,
     grad_o,
     grad_i,
     loc_sem,
@@ -253,6 +293,12 @@
         kap[x, Z0 + NZ : PZ, :] = zero_rows
         velyz[1, x - 1, 0:8, :] = zero_rows
         velyz[1, x - 1, Z0 + NZ : PZ, :] = zero_rows
+    for slot in range(7):
+        rim_f[slot, 0:8, :] = zero_rows
+        rim_f[slot, Z0 + NZ : PZ, :] = zero_rows
+    for slot in range(2):
+        rim_k[slot, 0:8, :] = zero_rows
+        rim_k[slot, Z0 + NZ : PZ, :] = zero_rows
     zero_plane = jnp.zeros((NZ, CY), F32)
 
     def zero_side(x):
@@ -265,12 +311,12 @@
     @pl.when(me_x == 0)
     def _():
         zero_side(0)
-        edge_d[...] = jnp.zeros_like(edge_d)
+        rim_d[...] = jnp.zeros_like(rim_d)
 
     @pl.when(me_x == gxn - 1)
     def _():
         zero_side(CX + 1)
-        edge_u[...] = jnp.zeros_like(edge_u)
+        rim_u[...] = jnp.zeros_like(rim_u)
 
     @pl.when(me_y == 0)
     def _():
@@ -283,11 +329,11 @@
     for load in loads[:4]:
         load.wait()
 
-    state_planes = [fields[0, s, 1 + x, mid, :] for s in range(2) for x in range(CX)]
-    edge_o[0] = pack_edges(state_planes)
-    coef_planes = [kap[1 + x, mid, :] for x in range(CX)]
-    coef_planes += [velyz[0, x, mid, :] for x in range(CX)]
-    edge_o[8] = pack_edges(coef_planes)
+    edge_o[0] = pack_cols([fields[0, s, 1 + x, mid, :] for s in range(2) for x in range(CX)])
+    edge_o[1] = pack_cols(
+        [kap[1 + x, mid, :] for x in range(CX)] + [velx[1 + x, mid, :] for x in range(CX)]
+    )
+    edge_o[2] = pack_cols([velyz[f, x, mid, :] for f in range(2) for x in range(CX)])
 
     pl.semaphore_wait(barrier, gyn - 1 + gxn - 1)
 
@@ -342,11 +388,11 @@
             device_id_type=MESH,
         )
 
-    def edge_x_copy(slot, side):
+    def rim_copy(slot, side):
         there = me_x - 1 if side == 0 else me_x + 1
-        sink = edge_u if side == 0 else edge_d
+        sink = rim_u if side == 0 else rim_d
         return pltpu.make_async_remote_copy(
-            src_ref=edge_o.at[slot],
+            src_ref=rim_o.at[slot, side],
             dst_ref=sink.at[slot],
             send_sem=fs_sem.at[slot, side],
             recv_sem=fr_sem.at[slot, side],
@@ -410,7 +456,7 @@
     def _(t):
         act_to(t).start()
 
-    both_sides(edge_copy, 1, start, (8, 0))
+    both_sides(edge_copy, 1, start, (1, 2, 0))
     both_sides(x_copy, 0, start, (8, 9, 0))
 
     @pl.loop(1, gyn)
@@ -421,12 +467,27 @@
     act_i[own_tile, :] = act_o[own_tile, :]
     sen_i[own_tile, :] = sen_o[own_tile, :]
 
+    def take_region(slot):
+        wait_recv(edge_copy, 1, (slot,))
+        return join_cols(edge_o[slot], edge_l[slot], edge_r[slot])
+
+    def send_rim(slot, region):
+        rim_o[slot, 0] = squeeze_x(region, 0)
+        rim_o[slot, 1] = squeeze_x(region, CX - 1)
+        both_sides(rim_copy, 0, start, (slot,))
+
+    def take_rim(slot, region):
+        wait_recv(rim_copy, 0, (slot,))
+        return beside_x(region, rim_d[slot], rim_u[slot])
+
+    region_a = take_region(1)
+    send_rim(1, region_a)
+    region_b = take_region(2)
+    rim_f[0, mid, :] = take_region(0)
+    send_rim(0, rim_f[0, mid, :])
+    halos = halo_planes(region_a, CX) + halo_planes(region_b, CX)
+    lane = iota((NZ, CY), 1)
     wait_recv(x_copy, 0, (8, 9))
-    wait_recv(edge_copy, 1, (8,))
-    halos = unpack_edges(merge_edges(edge_l[8], edge_r[8]), 2 * CX)
-    lane = iota((NZ, CY), 1)
-    rim_y = [[None] * (2 * CX) for _ in range(2)]
-    rim_x = [[None] * (2 * CX) for _ in range(2)]
     for x in range(CX):
         here = kap[1 + x, mid, :]
         kyp, kym = beside_y(here, halos[x])
@@ -467,19 +528,11 @@
                     cof[d, s, f, x] = parts[f]
                 cof[d, s, 2, x] = jnp.where(lane == CY - 1, 0.0, parts[2])
                 cof[d, s, 3, x] = jnp.where(lane == 0, 0.0, parts[3])
-                rim = jnp.where(lane == CY - 1, parts[2], jnp.where(lane == 0, parts[3], 0.0))
-                cof[d, s, 6, x] = rim
-                rim_y[d][s * CX + x] = rim
-                if x == 0:
-                    rim_x[d][s * CX + x] = parts[1]
-                if x == CX - 1:
-                    rim_x[d][s * CX + x] = parts[0]
-    for d in range(2):
-        pcy[d] = pack_edges(rim_y[d])
-        pcx[d] = pack_edges(rim_x[d])
+                cof[d, s, 6, x] = jnp.where(
+                    lane == CY - 1, parts[2], jnp.where(lane == 0, parts[3], 0.0)
+                )
 
     cells = [(s, x) for x in (0, CX - 1, 1, 2) for s in range(2)]
-    x_lane = lax.shift_right_logical(iota((8, CY), 1), 1) & (CX - 1)
 
     def base(slot, d, s, x):
         here = fields[slot, s, 1 + x, mid, :]
@@ -497,14 +550,9 @@
         return value
 
     def base_all(slot, d, extra):
-        planes = [None] * (2 * CX)
         for s, x in cells:
             value = base(slot, d, s, x)
-            if extra is not None:
-                value = value + extra(s, x)
-            bas[s, x] = value
-            planes[s * CX + x] = value
-        return planes
+            bas[s, x] = value if extra is None else value + extra(s, x)
 
     def finish(slot, d, s, x, halo):
         value = bas[s, x] + cof[d, s, 6, x] * halo
@@ -514,22 +562,15 @@
             value = value + cof[d, s, 0, x] * fields[slot, s, CX + 1, mid, :]
         return value
 
-    def take_y(slot):
-        wait_recv(edge_copy, 1, (slot,))
-        return merge_edges(edge_l[slot], edge_r[slot])
-
-    def next_edges(slot, d, rim, packed):
-        wait_recv(edge_x_copy, 0, (slot,))
-        across = jnp.where(
-            x_lane == 0, pltpu.roll(edge_d[slot], CY - 6, 1), pltpu.roll(edge_u[slot], 6, 1)
-        )
-        return packed + pcy[d] * rim + pcx[d] * across
-
-    def send_edges(slot, value):
-        edge_o[slot] = value
+    def finish_all(slot, d, region, put):
+        halos = halo_planes(region, 2 * CX)
+        wait_recv(x_copy, 0, (slot,))
+        for s, x in cells:
+            put(s, x, finish(slot, d, s, x, halos[s * CX + x]))
+
+    def send_cols(slot, planes):
+        edge_o[slot] = pack_cols(planes)
         both_sides(edge_copy, 1, start, (slot,))
-        if slot < 7:
-            both_sides(edge_x_copy, 0, start, (slot,))
 
     def put_field(slot, s, x, value):
         fields[slot, s, 1 + x, mid, :] = value
@@ -537,11 +578,73 @@
             both_sides(x_copy, 0, start, (slot,))
 
     base_all(0, 0, None)
-    rim = take_y(0)
-    wait_recv(x_copy, 0, (0,))
-    halos = unpack_edges(rim, 2 * CX)
-    for s, x in cells:
-        bas[s, x] = finish(0, 0, s, x, halos[s * CX + x])
+
+    def keep_base(s, x, value):
+        bas[s, x] = value
+
+    finish_all(0, 0, rim_f[0, mid, :], keep_base)
+
+    second = (lane & 32) != 0
+    outside = ((lane < 64) & ((lane & 7) < 4) & (me_y == 0)) | (
+        (lane >= 64) & ((lane & 7) >= 4) & (me_y == gyn - 1)
+    )
+    keep = jnp.where(outside, 0.0, 1.0)
+    scale_r = jnp.where(second, SCALES[1], SCALES[0])
+
+    def first_of(v):
+        return jnp.where(second, pltpu.roll(v, 32, 1), v)
+
+    def second_of(v):
+        return jnp.where(second, v, pltpu.roll(v, CY - 32, 1))
+
+    plus_a, minus_a = take_rim(1, region_a)
+    here = first_of(region_a)
+    rim_k[0, mid, :] = here
+    uz = second_of(region_b)
+    rim_k[1, mid, :] = uz
+    uy = first_of(region_b)
+    ux = second_of(region_a)
+    up, down = slice(Z0 + 1, Z0 + NZ + 1), slice(Z0 - 1, Z0 + NZ - 1)
+    around = (
+        first_of(plus_a),
+        first_of(minus_a),
+        pltpu.roll(here, CY - 1, 1),
+        pltpu.roll(here, 1, 1),
+        rim_k[0, up, :],
+        rim_k[0, down, :],
+    )
+    faces = [0.5 * (here + other) for other in around]
+    total = faces[0] + faces[1] + faces[2] + faces[3] + faces[4] + faces[5]
+    rim_c[0, 6] = keep * (1.0 - scale_r * total)
+    drifts = (
+        (-0.5 * ux, 0.5 * ux, -0.5 * uy, 0.5 * uy, -0.5 * uz, 0.5 * uz),
+        (
+            0.5 * second_of(plus_a),
+            -0.5 * second_of(minus_a),
+            0.5 * pltpu.roll(uy, CY - 1, 1),
+            -0.5 * pltpu.roll(uy, 1, 1),
+            0.5 * rim_k[1, up, :],
+            -0.5 * rim_k[1, down, :],
+        ),
+    )
+    for d in range(2):
+        for f in range(6):
+            rim_c[d, f] = keep * (scale_r * faces[f] + drifts[d][f])
+
+    def rim_step(slot, rim_slot, d):
+        region = rim_f[slot, mid, :]
+        plus, minus = take_rim(rim_slot, region)
+        return (
+            rim_c[0, 6] * region
+            + rim_c[d, 2] * pltpu.roll(region, CY - 1, 1)
+            + rim_c[d, 3] * pltpu.roll(region, 1, 1)
+            + rim_c[d, 4] * rim_f[slot, up, :]
+            + rim_c[d, 5] * rim_f[slot, down, :]
+            + rim_c[d, 0] * plus
+            + rim_c[d, 1] * minus
+        )
+
+    rim_f[1, mid, :] = rim_step(0, 0, 0)
 
     @pl.loop(1, gyn)
     def _(t):
@@ -603,13 +706,9 @@
                 row = bz * 32 + fx * 8
                 src[s, fx, bz * 8 : bz * 8 + 8, :] = placed[row : row + 8]
 
-    planes = [None] * (2 * CX)
+    send_cols(3, [src[s, x] for s in range(2) for x in range(CX)])
     for s, x in cells:
-        value = bas[s, x] + src[s, x]
-        planes[s * CX + x] = value
-        fields[1, s, 1 + x, mid, :] = value
-    send_edges(1, pack_edges(planes))
-    both_sides(x_copy, 0, start, (1,))
+        put_field(1, s, x, bas[s, x] + src[s, x])
 
     @pl.loop(1, gyn)
     def _(t):
@@ -636,15 +735,13 @@
     sn2_i[me_x] = sn2_o[me_x]
 
     supply = lambda s, x: src[s, x]
-    packed = pack_edges(base_all(1, 0, supply))
-
-    rim = take_y(1)
-    send_edges(2, next_edges(1, 0, rim, packed))
-    wait_recv(x_copy, 0, (1,))
-    halos = unpack_edges(rim, 2 * CX)
-    for s, x in cells:
-        put_field(2, s, x, finish(1, 0, s, x, halos[s * CX + x]))
-    packed = pack_edges(base_all(2, 0, supply))
+    base_all(1, 0, supply)
+
+    supply_r = take_region(3)
+    rim_f[1, mid, :] = rim_f[1, mid, :] + supply_r
+    send_rim(2, rim_f[1, mid, :])
+    finish_all(1, 0, rim_f[1, mid, :], lambda s, x, v: put_field(2, s, x, v))
+    base_all(2, 0, supply)
 
     @pl.loop(1, gxn)
     def _(t):
@@ -679,13 +776,10 @@
         for n in (4, 3):
             sensor_field(s * STEPS + n - 1)
 
-    rim = take_y(2)
-    send_edges(3, next_edges(2, 0, rim, packed))
-    wait_recv(x_copy, 0, (2,))
-    halos = unpack_edges(rim, 2 * CX)
-    for s, x in cells:
-        put_field(3, s, x, finish(2, 0, s, x, halos[s * CX + x]))
-    packed = pack_edges(base_all(3, 0, supply))
+    rim_f[2, mid, :] = rim_step(1, 2, 0) + supply_r
+    send_rim(3, rim_f[2, mid, :])
+    finish_all(2, 0, rim_f[2, mid, :], lambda s, x, v: put_field(3, s, x, v))
+    base_all(3, 0, supply)
 
     for s in range(2):
         for n in (2, 1):
@@ -698,38 +792,41 @@
         return cnt[span(x)] * state - obsf[s * STEPS + n - 1, span(x)]
 
     loads[4].wait()
-    packed_cnt = pack_edges([cnt[span(x)] for s in range(2) for x in range(CX)])
-    packed_goal = pack_edges(
-        [tgt[s, x] + obsf[s * STEPS + 3, span(x)] for s in range(2) for x in range(CX)]
-    )
-
-    rim = take_y(3)
-    edges = next_edges(3, 0, rim, packed)
-    send_edges(4, edges + packed_cnt * edges - packed_goal)
-    wait_recv(x_copy, 0, (3,))
-    halos = unpack_edges(rim, 2 * CX)
-    for s, x in cells:
-        value = finish(3, 0, s, x, halos[s * CX + x])
+    for n in (3, 2, 1):
+        send_cols(
+            3 + n,
+            [
+                forcing(fields[n, s, 1 + x, mid, :], s, x, n)
+                for s in range(2)
+                for x in range(CX)
+            ],
+        )
+
+    def last(s, x, value):
         out_c[s, x] = value
         adj = value - tgt[s, x] + forcing(value, s, x, 4)
         summed[s, x] = adj
         put_field(4, s, x, adj)
 
+    finish_all(3, 0, rim_step(2, 3, 0) + supply_r, last)
+    send_cols(7, [summed[s, x] for s in range(2) for x in range(CX)])
+
     for n in (3, 2, 1):
         slot = 7 - n
-        packed = pack_edges(
-            base_all(
-                slot, 1, lambda s, x: forcing(fields[n, s, 1 + x, mid, :], s, x, n)
-            )
-        )
-        rim = take_y(slot)
-        send_edges(slot + 1, next_edges(slot, 1, rim, packed))
-        wait_recv(x_copy, 0, (slot,))
-        halos = unpack_edges(rim, 2 * CX)
-        for s, x in cells:
-            adj = finish(slot, 1, s, x, halos[s * CX + x])
+        base_all(slot, 1, lambda s, x: forcing(fields[n, s, 1 + x, mid, :], s, x, n))
+        if n == 3:
+            region = take_region(7)
+        else:
+            pushed = take_region(4 + n)
+            region = rim_step(slot - 1, slot - 1, 1) + pushed
+        rim_f[slot, mid, :] = region
+        send_rim(slot, region)
+
+        def put(s, x, adj):
             summed[s, x] = summed[s, x] + adj
             put_field(slot + 1, s, x, adj)
+
+        finish_all(slot, 1, region, put)
 
     stacked = jnp.concatenate(
         [
@@ -766,11 +863,12 @@
     grad_i[own_tile, :] = grad_o[...]
 
     base_all(7, 1, None)
-    rim = take_y(7)
-    wait_recv(x_copy, 0, (7,))
-    halos = unpack_edges(rim, 2 * CX)
-    for s, x in cells:
-        out_s[s, x] = finish(7, 1, s, x, halos[s * CX + x])
+    region = rim_step(6, 6, 1) + take_region(4)
+
+    def keep_out(s, x, value):
+        out_s[s, x] = value
+
+    finish_all(7, 1, region, keep_out)
 
     @pl.loop(1, gyn)
     def _(t):
@@ -784,9 +882,9 @@
             jnp.where((slot_row & 7) == s, mine, 0.0), axis=0, keepdims=True
         )
 
-    both_sides(edge_copy, 1, wait_send, range(9))
+    both_sides(edge_copy, 1, wait_send, range(8))
     both_sides(x_copy, 0, wait_send, range(10))
-    both_sides(edge_x_copy, 0, wait_send, range(1, 7))
+    both_sides(rim_copy, 0, wait_send, range(7))
 
     @pl.loop(1, gyn)
     def _(t):
@@ -857,8 +955,9 @@
             pltpu.VMEM((2, CX, PZ, CY), F32),
             pltpu.VMEM((2, CX, NZ, CY), F32),
             pltpu.VMEM((2, 2, 8, CX, NZ, CY), F32),
-            pltpu.VMEM((2, 8, CY), F32),
-            pltpu.VMEM((2, 8, CY), F32),
+            pltpu.VMEM((7, PZ, CY), F32),
+            pltpu.VMEM((2, 7, NZ, CY), F32),
+            pltpu.VMEM((2, PZ, CY), F32),
             pltpu.VMEM((2, CX, NZ, CY), F32),
             pltpu.VMEM((2, CX, NZ, CY), F32),
             pltpu.VMEM((CX * NZ, CY), F32),
@@ -870,18 +969,19 @@
             pltpu.VMEM((rows, CY), F32),
             pltpu.VMEM((gxn, gyn, CY), F32),
             pltpu.VMEM((gxn, gyn, CY), F32),
-            pltpu.VMEM((9, 8, CY), F32),
-            pltpu.VMEM((9, 8, CY), F32),
-            pltpu.VMEM((9, 8, CY), F32),
-            pltpu.VMEM((7, 8, CY), F32),
-            pltpu.VMEM((7, 8, CY), F32),
+            pltpu.VMEM((8, NZ // 2, CY), F32),
+            pltpu.VMEM((8, NZ // 2, CY), F32),
+            pltpu.VMEM((8, NZ // 2, CY), F32),
+            pltpu.VMEM((7, 2, 16, CY), F32),
+            pltpu.VMEM((7, 16, CY), F32),
+            pltpu.VMEM((7, 16, CY), F32),
             pltpu.VMEM((8, CY), F32),
             pltpu.VMEM((rows, CY), F32),
             dma((12,)),
             dma((10, 2)),
             dma((10, 2)),
-            dma((9, 2)),
-            dma((9, 2)),
+            dma((8, 2)),
+            dma((8, 2)),
             dma((7, 2)),
             dma((7, 2)),
             dma((gyn,)),

time: 44.6 us -> 42 us (0.942)
  Pallas kernels: 43.6 us -> 41.2 us
    pallas_call x1, Pallas kernels: 42.9 us -> 40.4 us  [per_device(): pl.pallas_call(functools.partial(whole_kernel, gxn, gyn), out_shape=(pltp...]
where the time goes in v3:
time: 42 us; the launch traced here: 41.8 us
  Pallas kernels  41.2 us (98%)
  between operations  0.64 us (2%)
    pallas_call x1, Pallas kernels, per_device(): pl.pallas_call(functools.partial(whole_kernel, gxn, gyn), out_shape=(pltp...  40.4 us

profile of v3, /device:TPU:1, one launch (start us, length us, event | category | flops | bytes accessed | tf_op | source)
XLA Modules:
  0.0 41.8 jit_solution(6088125252581704934)
XLA Ops:
  0.6 40.4 %whole.1 = (f32[2,4,48,128]{3,2,1,0:T(8,128)S(1)}, f32[2,4,48,128]{3,2,1,0:T(8,128)S(1)}, f32[2,32]{1,0:T(2,128)S(1)}) custom-call(f32[2,4,48,128]{3,2,1,0:T(8,128)} %c0_h.1, f32[4,48,128]{2,1,0:T(8,128)} %kap_h.1, f32[3,4,48,128]{3,2,1,0:T(8,128)} %vel_h.1, f32[2,4,48,128]{3,2,1,0:T(8,128)} %tgt_h.1, s32[1,256]{1,0:T(1,128)} %bitcast.8, s32[1,256]{1,0:T(1,128)} %bitcast.9, ...), custom_call_target="tpu_custom_call" | custom-call | tf_op jit(solution)/shard_map/whole/pallas_call | solution.py:935
  41.1 0.8 %store.1 = (f32[2,4,48,128]{3,2,1,0:T(8,128)}, f32[2,4,48,128]{3,2,1,0:T(8,128)}, f32[2,32]{1,0:T(2,128)}) custom-call(f32[2,4,48,128]{3,2,1,0:T(8,128)S(1)} %get-tuple-element.9.state, f32[2,4,48,128]{3,2,1,0:T(8,128)S(1)} %get-tuple-element.10.sensitivity, f32[2,32]{1,0:T(2,128)S(1)} %get-tuple-element.11.gradient), custom_call_target="tpu_custom_call" | custom-call | tf_op jit(solution)/shard_map/store/pallas_call | solution.py:1013

commit v4 on v3

--- a/solution.py
+++ b/solution.py
@@ -23,6 +23,7 @@
 ZV = NZ // 8
 PZ = NZ + 16
 Z0 = 8
+PART = NZ // 2
 prandtl = 0.85
 SCALES = (1.0, 1.0 / prandtl)
 
@@ -335,6 +336,28 @@
     )
     edge_o[2] = pack_cols([velyz[f, x, mid, :] for f in range(2) for x in range(CX)])
 
+    cells = [(s, x) for x in (0, CX - 1, 1, 2) for s in range(2)]
+
+    def base(slot, d, s, x):
+        here = fields[slot, s, 1 + x, mid, :]
+        value = (
+            cof[0, s, 7, x] * here
+            + cof[d, s, 2, x] * pltpu.roll(here, CY - 1, 1)
+            + cof[d, s, 3, x] * pltpu.roll(here, 1, 1)
+            + cof[d, s, 4, x] * fields[slot, s, 1 + x, Z0 + 1 : Z0 + NZ + 1, :]
+            + cof[d, s, 5, x] * fields[slot, s, 1 + x, Z0 - 1 : Z0 + NZ - 1, :]
+        )
+        if x < CX - 1:
+            value = value + cof[d, s, 0, x] * fields[slot, s, 2 + x, mid, :]
+        if x > 0:
+            value = value + cof[d, s, 1, x] * fields[slot, s, x, mid, :]
+        return value
+
+    def base_all(slot, d, extra):
+        for s, x in cells:
+            value = base(slot, d, s, x)
+            bas[s, x] = value if extra is None else value + extra(s, x)
+
     pl.semaphore_wait(barrier, gyn - 1 + gxn - 1)
 
     def to_peer_y(source, sink, send, recv):
@@ -400,27 +423,23 @@
             device_id_type=MESH,
         )
 
-    def x_copy(slot, side):
+    def x_copy(slot, side, chunk=0):
         there = me_x - 1 if side == 0 else me_x + 1
         sink = CX + 1 if side == 0 else 0
         own = 0 if side == 0 else CX - 1
-        if slot == 0:
-            source = c0_h.at[:, own]
-            dest = fields.at[0, :, sink, mid, :]
-        elif slot < 8:
-            source = fields.at[slot, :, own + 1, mid, :]
-            dest = fields.at[slot, :, sink, mid, :]
-        elif slot == 8:
-            source = kap_h.at[own]
-            dest = kap.at[sink, mid, :]
+        part = slice(Z0 + PART * (chunk % 2), Z0 + PART * (chunk % 2 + 1))
+        if slot < 8:
+            source = fields.at[slot, chunk // 2, own + 1, part, :]
+            dest = fields.at[slot, chunk // 2, sink, part, :]
         else:
-            source = vel_h.at[0, own]
-            dest = velx.at[sink, mid, :]
+            held = kap if slot == 8 else velx
+            source = held.at[own + 1, part, :]
+            dest = held.at[sink, part, :]
         return pltpu.make_async_remote_copy(
             src_ref=source,
             dst_ref=dest,
-            send_sem=xs_sem.at[slot, side],
-            recv_sem=xr_sem.at[slot, side],
+            send_sem=xs_sem.at[slot, side, chunk],
+            recv_sem=xr_sem.at[slot, side, chunk],
             device_id=(there, me_y),
             device_id_type=MESH,
         )
@@ -452,12 +471,16 @@
                 for slot in slots:
                     maker(slot, side).wait_recv()
 
+    for chunk in range(2):
+        both_sides(lambda a, b: x_copy(a, b, chunk), 0, start, (8, 9))
+    for chunk in range(4):
+        both_sides(lambda a, b: x_copy(a, b, chunk), 0, start, (0,))
+
     @pl.loop(1, gyn)
     def _(t):
         act_to(t).start()
 
     both_sides(edge_copy, 1, start, (1, 2, 0))
-    both_sides(x_copy, 0, start, (8, 9, 0))
 
     @pl.loop(1, gyn)
     def _(t):
@@ -466,6 +489,51 @@
     own_tile = pl.ds(pl.multiple_of(me_y * 8, 8), 8)
     act_i[own_tile, :] = act_o[own_tile, :]
     sen_i[own_tile, :] = sen_o[own_tile, :]
+
+    lane = iota((NZ, CY), 1)
+    nothing = jnp.zeros((NZ, CY), F32)
+    for x in range(CX):
+        here = kap[1 + x, mid, :]
+        kyp, kym = beside_y(here, nothing)
+        around = (
+            kap[2 + x, mid, :] if x < CX - 1 else nothing,
+            kap[x, mid, :] if x > 0 else nothing,
+            kyp,
+            kym,
+            kap[1 + x, Z0 + 1 : Z0 + NZ + 1, :],
+            kap[1 + x, Z0 - 1 : Z0 + NZ - 1, :],
+        )
+        faces = [0.5 * (here + other) for other in around]
+        total = faces[0] + faces[1] + faces[2] + faces[3] + faces[4] + faces[5]
+        uy = velyz[0, x, mid, :]
+        uyp, uym = beside_y(uy, nothing)
+        ux = velx[1 + x, mid, :]
+        uz = velyz[1, x, mid, :]
+        drifts = (
+            (-0.5 * ux, 0.5 * ux, -0.5 * uy, 0.5 * uy, -0.5 * uz, 0.5 * uz),
+            (
+                0.5 * velx[2 + x, mid, :] if x < CX - 1 else None,
+                -0.5 * velx[x, mid, :] if x > 0 else None,
+                0.5 * uyp,
+                -0.5 * uym,
+                0.5 * velyz[1, x, Z0 + 1 : Z0 + NZ + 1, :],
+                -0.5 * velyz[1, x, Z0 - 1 : Z0 + NZ - 1, :],
+            ),
+        )
+        for s in range(2):
+            scale = SCALES[s]
+            cof[0, s, 7, x] = 1.0 - scale * total
+            for d in range(2):
+                for f in range(6):
+                    if (f == 0 and x == CX - 1) or (f == 1 and x == 0):
+                        continue
+                    part = (faces[f] if s == 0 else scale * faces[f]) + drifts[d][f]
+                    if f == 2:
+                        part = jnp.where(lane == CY - 1, 0.0, part)
+                    if f == 3:
+                        part = jnp.where(lane == 0, 0.0, part)
+                    cof[d, s, f, x] = part
+    base_all(0, 0, None)
 
     def take_region(slot):
         wait_recv(edge_copy, 1, (slot,))
@@ -486,165 +554,9 @@
     rim_f[0, mid, :] = take_region(0)
     send_rim(0, rim_f[0, mid, :])
     halos = halo_planes(region_a, CX) + halo_planes(region_b, CX)
-    lane = iota((NZ, CY), 1)
-    wait_recv(x_copy, 0, (8, 9))
-    for x in range(CX):
-        here = kap[1 + x, mid, :]
-        kyp, kym = beside_y(here, halos[x])
-        around = (
-            kap[2 + x, mid, :],
-            kap[x, mid, :],
-            kyp,
-            kym,
-            kap[1 + x, Z0 + 1 : Z0 + NZ + 1, :],
-            kap[1 + x, Z0 - 1 : Z0 + NZ - 1, :],
-        )
-        faces = [0.5 * (here + other) for other in around]
-        total = faces[0] + faces[1] + faces[2] + faces[3] + faces[4] + faces[5]
-        uy = velyz[0, x, mid, :]
-        uyp, uym = beside_y(uy, halos[CX + x])
-        ux = velx[1 + x, mid, :]
-        uz = velyz[1, x, mid, :]
-        drifts = (
-            (-0.5 * ux, 0.5 * ux, -0.5 * uy, 0.5 * uy, -0.5 * uz, 0.5 * uz),
-            (
-                0.5 * velx[2 + x, mid, :],
-                -0.5 * velx[x, mid, :],
-                0.5 * uyp,
-                -0.5 * uym,
-                0.5 * velyz[1, x, Z0 + 1 : Z0 + NZ + 1, :],
-                -0.5 * velyz[1, x, Z0 - 1 : Z0 + NZ - 1, :],
-            ),
-        )
-        for s in range(2):
-            scale = SCALES[s]
-            cof[0, s, 7, x] = 1.0 - scale * total
-            for d in range(2):
-                parts = []
-                for f in range(6):
-                    scaled = faces[f] if s == 0 else scale * faces[f]
-                    parts.append(scaled + drifts[d][f])
-                for f in (0, 1, 4, 5):
-                    cof[d, s, f, x] = parts[f]
-                cof[d, s, 2, x] = jnp.where(lane == CY - 1, 0.0, parts[2])
-                cof[d, s, 3, x] = jnp.where(lane == 0, 0.0, parts[3])
-                cof[d, s, 6, x] = jnp.where(
-                    lane == CY - 1, parts[2], jnp.where(lane == 0, parts[3], 0.0)
-                )
-
-    cells = [(s, x) for x in (0, CX - 1, 1, 2) for s in range(2)]
-
-    def base(slot, d, s, x):
-        here = fields[slot, s, 1 + x, mid, :]
-        value = (
-            cof[0, s, 7, x] * here
-            + cof[d, s, 2, x] * pltpu.roll(here, CY - 1, 1)
-            + cof[d, s, 3, x] * pltpu.roll(here, 1, 1)
-            + cof[d, s, 4, x] * fields[slot, s, 1 + x, Z0 + 1 : Z0 + NZ + 1, :]
-            + cof[d, s, 5, x] * fields[slot, s, 1 + x, Z0 - 1 : Z0 + NZ - 1, :]
-        )
-        if x < CX - 1:
-            value = value + cof[d, s, 0, x] * fields[slot, s, 2 + x, mid, :]
-        if x > 0:
-            value = value + cof[d, s, 1, x] * fields[slot, s, x, mid, :]
-        return value
-
-    def base_all(slot, d, extra):
-        for s, x in cells:
-            value = base(slot, d, s, x)
-            bas[s, x] = value if extra is None else value + extra(s, x)
-
-    def finish(slot, d, s, x, halo):
-        value = bas[s, x] + cof[d, s, 6, x] * halo
-        if x == 0:
-            value = value + cof[d, s, 1, x] * fields[slot, s, 0, mid, :]
-        if x == CX - 1:
-            value = value + cof[d, s, 0, x] * fields[slot, s, CX + 1, mid, :]
-        return value
-
-    def finish_all(slot, d, region, put):
-        halos = halo_planes(region, 2 * CX)
-        wait_recv(x_copy, 0, (slot,))
-        for s, x in cells:
-            put(s, x, finish(slot, d, s, x, halos[s * CX + x]))
-
     def send_cols(slot, planes):
         edge_o[slot] = pack_cols(planes)
         both_sides(edge_copy, 1, start, (slot,))
-
-    def put_field(slot, s, x, value):
-        fields[slot, s, 1 + x, mid, :] = value
-        if x == CX - 1 and s == 1:
-            both_sides(x_copy, 0, start, (slot,))
-
-    base_all(0, 0, None)
-
-    def keep_base(s, x, value):
-        bas[s, x] = value
-
-    finish_all(0, 0, rim_f[0, mid, :], keep_base)
-
-    second = (lane & 32) != 0
-    outside = ((lane < 64) & ((lane & 7) < 4) & (me_y == 0)) | (
-        (lane >= 64) & ((lane & 7) >= 4) & (me_y == gyn - 1)
-    )
-    keep = jnp.where(outside, 0.0, 1.0)
-    scale_r = jnp.where(second, SCALES[1], SCALES[0])
-
-    def first_of(v):
-        return jnp.where(second, pltpu.roll(v, 32, 1), v)
-
-    def second_of(v):
-        return jnp.where(second, v, pltpu.roll(v, CY - 32, 1))
-
-    plus_a, minus_a = take_rim(1, region_a)
-    here = first_of(region_a)
-    rim_k[0, mid, :] = here
-    uz = second_of(region_b)
-    rim_k[1, mid, :] = uz
-    uy = first_of(region_b)
-    ux = second_of(region_a)
-    up, down = slice(Z0 + 1, Z0 + NZ + 1), slice(Z0 - 1, Z0 + NZ - 1)
-    around = (
-        first_of(plus_a),
-        first_of(minus_a),
-        pltpu.roll(here, CY - 1, 1),
-        pltpu.roll(here, 1, 1),
-        rim_k[0, up, :],
-        rim_k[0, down, :],
-    )
-    faces = [0.5 * (here + other) for other in around]
-    total = faces[0] + faces[1] + faces[2] + faces[3] + faces[4] + faces[5]
-    rim_c[0, 6] = keep * (1.0 - scale_r * total)
-    drifts = (
-        (-0.5 * ux, 0.5 * ux, -0.5 * uy, 0.5 * uy, -0.5 * uz, 0.5 * uz),
-        (
-            0.5 * second_of(plus_a),
-            -0.5 * second_of(minus_a),
-            0.5 * pltpu.roll(uy, CY - 1, 1),
-            -0.5 * pltpu.roll(uy, 1, 1),
-            0.5 * rim_k[1, up, :],
-            -0.5 * rim_k[1, down, :],
-        ),
-    )
-    for d in range(2):
-        for f in range(6):
-            rim_c[d, f] = keep * (scale_r * faces[f] + drifts[d][f])
-
-    def rim_step(slot, rim_slot, d):
-        region = rim_f[slot, mid, :]
-        plus, minus = take_rim(rim_slot, region)
-        return (
-            rim_c[0, 6] * region
-            + rim_c[d, 2] * pltpu.roll(region, CY - 1, 1)
-            + rim_c[d, 3] * pltpu.roll(region, 1, 1)
-            + rim_c[d, 4] * rim_f[slot, up, :]
-            + rim_c[d, 5] * rim_f[slot, down, :]
-            + rim_c[d, 0] * plus
-            + rim_c[d, 1] * minus
-        )
-
-    rim_f[1, mid, :] = rim_step(0, 0, 0)
 
     @pl.loop(1, gyn)
     def _(t):
@@ -707,8 +619,140 @@
                 src[s, fx, bz * 8 : bz * 8 + 8, :] = placed[row : row + 8]
 
     send_cols(3, [src[s, x] for s in range(2) for x in range(CX)])
-    for s, x in cells:
-        put_field(1, s, x, bas[s, x] + src[s, x])
+    for chunk in range(2):
+        wait_recv(lambda a, b: x_copy(a, b, chunk), 0, (8, 9))
+    sign_y = jnp.where(lane == CY - 1, 1.0, jnp.where(lane == 0, -1.0, 0.0))
+    on_y = sign_y != 0.0
+    for x in range(CX):
+        here = kap[1 + x, mid, :]
+        missing = jnp.where(on_y, 0.5 * halos[x], 0.0)
+        face_y = jnp.where(on_y, 0.5 * (here + halos[x]), 0.0)
+        drift_y = (
+            -0.5 * sign_y * velyz[0, x, mid, :],
+            0.5 * sign_y * halos[CX + x],
+        )
+        if x in (0, CX - 1):
+            far = 0 if x == 0 else CX + 1
+            sign = -0.5 if x == 0 else 0.5
+            missing = missing + 0.5 * kap[far, mid, :]
+            face_x = 0.5 * (here + kap[far, mid, :])
+            drift_x = (-sign * velx[1 + x, mid, :], sign * velx[far, mid, :])
+        for s in range(2):
+            scaled = missing if s == 0 else SCALES[s] * missing
+            cof[0, s, 7, x] = cof[0, s, 7, x] - scaled
+            bas[s, x] = bas[s, x] - scaled * fields[0, s, 1 + x, mid, :]
+            for d in range(2):
+                cof[d, s, 6, x] = SCALES[s] * face_y + drift_y[d]
+                if x in (0, CX - 1):
+                    cof[d, s, 1 if x == 0 else 0, x] = SCALES[s] * face_x + drift_x[d]
+
+    whole = slice(0, NZ)
+
+    def finish(slot, d, s, x, halo, part):
+        value = bas[s, x, part] + cof[d, s, 6, x, part] * halo[part]
+        far = slice(Z0 + part.start, Z0 + part.stop)
+        if x == 0:
+            value = value + cof[d, s, 1, x, part] * fields[slot, s, 0, far, :]
+        if x == CX - 1:
+            value = value + cof[d, s, 0, x, part] * fields[slot, s, CX + 1, far, :]
+        return value
+
+    def put_field(slot, s, x, part, value):
+        fields[slot, s, 1 + x, slice(Z0 + part.start, Z0 + part.stop), :] = value
+
+    def send_chunk(slot, chunk):
+        both_sides(lambda a, b: x_copy(a, b, chunk), 0, start, (slot,))
+
+    def finish_all(slot, d, region, put, onward):
+        halos = halo_planes(region, 2 * CX)
+        for chunk in range(4):
+            s, z = chunk // 2, chunk % 2
+            part = slice(z * PART, z * PART + PART)
+            wait_recv(lambda a, b: x_copy(a, b, chunk), 0, (slot,))
+            for x in (0, CX - 1):
+                put(s, x, part, finish(slot, d, s, x, halos[s * CX + x], part))
+            if onward:
+                send_chunk(onward, chunk)
+        for s in range(2):
+            for x in range(1, CX - 1):
+                put(s, x, whole, finish(slot, d, s, x, halos[s * CX + x], whole))
+
+    def keep_base(s, x, part, value):
+        bas[s, x, part] = value
+
+    finish_all(0, 0, rim_f[0, mid, :], keep_base, 0)
+
+    for chunk in range(4):
+        s, z = chunk // 2, chunk % 2
+        part = slice(z * PART, z * PART + PART)
+        for x in (0, CX - 1):
+            put_field(1, s, x, part, bas[s, x, part] + src[s, x, part])
+        send_chunk(1, chunk)
+    for s in range(2):
+        for x in range(1, CX - 1):
+            put_field(1, s, x, whole, bas[s, x] + src[s, x])
+
+    second = (lane & 32) != 0
+    outside = ((lane < 64) & ((lane & 7) < 4) & (me_y == 0)) | (
+        (lane >= 64) & ((lane & 7) >= 4) & (me_y == gyn - 1)
+    )
+    keep = jnp.where(outside, 0.0, 1.0)
+    scale_r = jnp.where(second, SCALES[1], SCALES[0])
+
+    def first_of(v):
+        return jnp.where(second, pltpu.roll(v, 32, 1), v)
+
+    def second_of(v):
+        return jnp.where(second, v, pltpu.roll(v, CY - 32, 1))
+
+    plus_a, minus_a = take_rim(1, region_a)
+    here = first_of(region_a)
+    rim_k[0, mid, :] = here
+    uz = second_of(region_b)
+    rim_k[1, mid, :] = uz
+    uy = first_of(region_b)
+    ux = second_of(region_a)
+    up, down = slice(Z0 + 1, Z0 + NZ + 1), slice(Z0 - 1, Z0 + NZ - 1)
+    around = (
+        first_of(plus_a),
+        first_of(minus_a),
+        pltpu.roll(here, CY - 1, 1),
+        pltpu.roll(here, 1, 1),
+        rim_k[0, up, :],
+        rim_k[0, down, :],
+    )
+    faces = [0.5 * (here + other) for other in around]
+    total = faces[0] + faces[1] + faces[2] + faces[3] + faces[4] + faces[5]
+    rim_c[0, 6] = keep * (1.0 - scale_r * total)
+    drifts = (
+        (-0.5 * ux, 0.5 * ux, -0.5 * uy, 0.5 * uy, -0.5 * uz, 0.5 * uz),
+        (
+            0.5 * second_of(plus_a),
+            -0.5 * second_of(minus_a),
+            0.5 * pltpu.roll(uy, CY - 1, 1),
+            -0.5 * pltpu.roll(uy, 1, 1),
+            0.5 * rim_k[1, up, :],
+            -0.5 * rim_k[1, down, :],
+        ),
+    )
+    for d in range(2):
+        for f in range(6):
+            rim_c[d, f] = keep * (scale_r * faces[f] + drifts[d][f])
+
+    def rim_step(slot, rim_slot, d):
+        region = rim_f[slot, mid, :]
+        plus, minus = take_rim(rim_slot, region)
+        return (
+            rim_c[0, 6] * region
+            + rim_c[d, 2] * pltpu.roll(region, CY - 1, 1)
+            + rim_c[d, 3] * pltpu.roll(region, 1, 1)
+            + rim_c[d, 4] * rim_f[slot, up, :]
+            + rim_c[d, 5] * rim_f[slot, down, :]
+            + rim_c[d, 0] * plus
+            + rim_c[d, 1] * minus
+        )
+
+    rim_f[1, mid, :] = rim_step(0, 0, 0)
 
     @pl.loop(1, gyn)
     def _(t):
@@ -740,7 +784,7 @@
     supply_r = take_region(3)
     rim_f[1, mid, :] = rim_f[1, mid, :] + supply_r
     send_rim(2, rim_f[1, mid, :])
-    finish_all(1, 0, rim_f[1, mid, :], lambda s, x, v: put_field(2, s, x, v))
+    finish_all(1, 0, rim_f[1, mid, :], functools.partial(put_field, 2), 2)
     base_all(2, 0, supply)
 
     @pl.loop(1, gxn)
@@ -773,17 +817,15 @@
         obsf[ch] = o0 + o1 + o2
 
     for s in range(2):
-        for n in (4, 3):
-            sensor_field(s * STEPS + n - 1)
+        sensor_field(s * STEPS + 3)
 
     rim_f[2, mid, :] = rim_step(1, 2, 0) + supply_r
     send_rim(3, rim_f[2, mid, :])
-    finish_all(2, 0, rim_f[2, mid, :], lambda s, x, v: put_field(3, s, x, v))
+    finish_all(2, 0, rim_f[2, mid, :], functools.partial(put_field, 3), 3)
     base_all(3, 0, supply)
 
     for s in range(2):
-        for n in (2, 1):
-            sensor_field(s * STEPS + n - 1)
+        sensor_field(s * STEPS + 2)
 
     def span(x):
         return slice(x * NZ, x * NZ + NZ)
@@ -792,7 +834,7 @@
         return cnt[span(x)] * state - obsf[s * STEPS + n - 1, span(x)]
 
     loads[4].wait()
-    for n in (3, 2, 1):
+    def send_forcing(n):
         send_cols(
             3 + n,
             [
@@ -802,18 +844,26 @@
             ],
         )
 
-    def last(s, x, value):
-        out_c[s, x] = value
-        adj = value - tgt[s, x] + forcing(value, s, x, 4)
-        summed[s, x] = adj
-        put_field(4, s, x, adj)
-
-    finish_all(3, 0, rim_step(2, 3, 0) + supply_r, last)
+    send_forcing(3)
+
+    def last(s, x, part, value):
+        out_c[s, x, part] = value
+        flat = slice(x * NZ + part.start, x * NZ + part.stop)
+        push = cnt[flat] * value - obsf[s * STEPS + 3, flat]
+        adj = value - tgt[s, x, part] + push
+        summed[s, x, part] = adj
+        put_field(4, s, x, part, adj)
+
+    finish_all(3, 0, rim_step(2, 3, 0) + supply_r, last, 4)
     send_cols(7, [summed[s, x] for s in range(2) for x in range(CX)])
 
     for n in (3, 2, 1):
         slot = 7 - n
         base_all(slot, 1, lambda s, x: forcing(fields[n, s, 1 + x, mid, :], s, x, n))
+        if n > 1:
+            for s in range(2):
+                sensor_field(s * STEPS + n - 2)
+            send_forcing(n - 1)
         if n == 3:
             region = take_region(7)
         else:
@@ -822,11 +872,11 @@
         rim_f[slot, mid, :] = region
         send_rim(slot, region)
 
-        def put(s, x, adj):
-            summed[s, x] = summed[s, x] + adj
-            put_field(slot + 1, s, x, adj)
-
-        finish_all(slot, 1, region, put)
+        def put(s, x, part, adj):
+            summed[s, x, part] = summed[s, x, part] + adj
+            put_field(slot + 1, s, x, part, adj)
+
+        finish_all(slot, 1, region, put, slot + 1)
 
     stacked = jnp.concatenate(
         [
@@ -865,10 +915,26 @@
     base_all(7, 1, None)
     region = rim_step(6, 6, 1) + take_region(4)
 
-    def keep_out(s, x, value):
-        out_s[s, x] = value
-
-    finish_all(7, 1, region, keep_out)
+    def keep_out(s, x, part, value):
+        out_s[s, x, part] = value
+
+    finish_all(7, 1, region, keep_out, 0)
+
+    both_sides(edge_copy, 1, wait_send, range(8))
+    both_sides(x_copy, 0, wait_send, range(10))
+    both_sides(lambda a, b: x_copy(a, b, 1), 0, wait_send, range(10))
+    for chunk in range(2, 4):
+        both_sides(lambda a, b: x_copy(a, b, chunk), 0, wait_send, range(8))
+    both_sides(rim_copy, 0, wait_send, range(7))
+
+    @pl.loop(1, gyn)
+    def _(t):
+        act_to(t).wait_send()
+        sen_to(t).wait_send()
+
+    @pl.loop(1, gxn)
+    def _(t):
+        sn2_copy(t, True).wait_send()
 
     @pl.loop(1, gyn)
     def _(t):
@@ -882,19 +948,9 @@
             jnp.where((slot_row & 7) == s, mine, 0.0), axis=0, keepdims=True
         )
 
-    both_sides(edge_copy, 1, wait_send, range(8))
-    both_sides(x_copy, 0, wait_send, range(10))
-    both_sides(rim_copy, 0, wait_send, range(7))
-
     @pl.loop(1, gyn)
     def _(t):
-        act_to(t).wait_send()
-        sen_to(t).wait_send()
         grad_to(t).wait_send()
-
-    @pl.loop(1, gxn)
-    def _(t):
-        sn2_copy(t, True).wait_send()
 
 
 def store_kernel(state, sensitivity, gradient, out_c, out_s, out_g, sem):
@@ -978,8 +1034,8 @@
             pltpu.VMEM((8, CY), F32),
             pltpu.VMEM((rows, CY), F32),
             dma((12,)),
-            dma((10, 2)),
-            dma((10, 2)),
+            dma((10, 2, 4)),
+            dma((10, 2, 4)),
             dma((8, 2)),
             dma((8, 2)),
             dma((7, 2)),

time: 42 us -> 40.8 us (0.971)
  Pallas kernels: 41.2 us -> 40 us
    pallas_call x1, Pallas kernels: 40.4 us -> 39.2 us  [per_device(): pl.pallas_call(functools.partial(whole_kernel, gxn, gyn), out_shape=(pltp...]
where the time goes in v4:
time: 40.8 us; the launch traced here: 40.6 us
  Pallas kernels  40 us (98%)
  between operations  0.64 us (2%)
    pallas_call x1, Pallas kernels, per_device(): pl.pallas_call(functools.partial(whole_kernel, gxn, gyn), out_shape=(pltp...  39.2 us

profile of v4, /device:TPU:1, one launch (start us, length us, event | category | flops | bytes accessed | tf_op | source)
XLA Modules:
  0.0 40.6 jit_solution(10493368837404149410)
XLA Ops:
  0.6 39.2 %whole.1 = (f32[2,4,48,128]{3,2,1,0:T(8,128)S(1)}, f32[2,4,48,128]{3,2,1,0:T(8,128)S(1)}, f32[2,32]{1,0:T(2,128)S(1)}) custom-call(f32[2,4,48,128]{3,2,1,0:T(8,128)} %c0_h.1, f32[4,48,128]{2,1,0:T(8,128)} %kap_h.1, f32[3,4,48,128]{3,2,1,0:T(8,128)} %vel_h.1, f32[2,4,48,128]{3,2,1,0:T(8,128)} %tgt_h.1, s32[1,256]{1,0:T(1,128)} %bitcast.8, s32[1,256]{1,0:T(1,128)} %bitcast.9, ...), custom_call_target="tpu_custom_call" | custom-call | tf_op jit(solution)/shard_map/whole/pallas_call | solution.py:991
  39.9 0.8 %store.1 = (f32[2,4,48,128]{3,2,1,0:T(8,128)}, f32[2,4,48,128]{3,2,1,0:T(8,128)}, f32[2,32]{1,0:T(2,128)}) custom-call(f32[2,4,48,128]{3,2,1,0:T(8,128)S(1)} %get-tuple-element.9.state, f32[2,4,48,128]{3,2,1,0:T(8,128)S(1)} %get-tuple-element.10.sensitivity, f32[2,32]{1,0:T(2,128)S(1)} %get-tuple-element.11.gradient), custom_call_target="tpu_custom_call" | custom-call | tf_op jit(solution)/shard_map/store/pallas_call | solution.py:1069

commit v5 on v4

--- a/solution.py
+++ b/solution.py
@@ -23,7 +23,6 @@
 ZV = NZ // 8
 PZ = NZ + 16
 Z0 = 8
-PART = NZ // 2
 prandtl = 0.85
 SCALES = (1.0, 1.0 / prandtl)
 
@@ -205,6 +204,17 @@
     lg_y = gyn.bit_length() - 1
     mid = slice(Z0, Z0 + NZ)
 
+    far_first = [t for t in (10, 6, 9, 11, 14, 7, 5, 13, 8, 2, 3, 12, 15, 4, 1) if t < gyn]
+    barrier = pltpu.get_barrier_semaphore()
+    for t in far_first:
+        pl.semaphore_signal(
+            barrier, inc=1, device_id=(me_x, lax.rem(me_y + t, gyn)), device_id_type=MESH
+        )
+    for t in range(1, gxn):
+        pl.semaphore_signal(
+            barrier, inc=1, device_id=(lax.rem(me_x + t, gxn), me_y), device_id_type=MESH
+        )
+
     smalls = [
         pltpu.make_async_copy(source, sink, loc_sem.at[5 + i])
         for i, (source, sink) in enumerate(
@@ -230,20 +240,6 @@
     ]
     for load in loads:
         load.start()
-
-    barrier = pltpu.get_barrier_semaphore()
-
-    @pl.loop(1, gyn)
-    def _(t):
-        pl.semaphore_signal(
-            barrier, inc=1, device_id=(me_x, lax.rem(me_y + t, gyn)), device_id_type=MESH
-        )
-
-    @pl.loop(1, gxn)
-    def _(t):
-        pl.semaphore_signal(
-            barrier, inc=1, device_id=(lax.rem(me_x + t, gxn), me_y), device_id_type=MESH
-        )
 
     for load in smalls:
         load.wait()
@@ -427,10 +423,10 @@
         there = me_x - 1 if side == 0 else me_x + 1
         sink = CX + 1 if side == 0 else 0
         own = 0 if side == 0 else CX - 1
-        part = slice(Z0 + PART * (chunk % 2), Z0 + PART * (chunk % 2 + 1))
+        part = mid
         if slot < 8:
-            source = fields.at[slot, chunk // 2, own + 1, part, :]
-            dest = fields.at[slot, chunk // 2, sink, part, :]
+            source = fields.at[slot, chunk, own + 1, part, :]
+            dest = fields.at[slot, chunk, sink, part, :]
         else:
             held = kap if slot == 8 else velx
             source = held.at[own + 1, part, :]
@@ -471,13 +467,12 @@
                 for slot in slots:
                     maker(slot, side).wait_recv()
 
+    both_sides(x_copy, 0, start, (8,))
     for chunk in range(2):
-        both_sides(lambda a, b: x_copy(a, b, chunk), 0, start, (8, 9))
-    for chunk in range(4):
         both_sides(lambda a, b: x_copy(a, b, chunk), 0, start, (0,))
-
-    @pl.loop(1, gyn)
-    def _(t):
+    both_sides(x_copy, 0, start, (9,))
+
+    for t in far_first:
         act_to(t).start()
 
     both_sides(edge_copy, 1, start, (1, 2, 0))
@@ -619,8 +614,7 @@
                 src[s, fx, bz * 8 : bz * 8 + 8, :] = placed[row : row + 8]
 
     send_cols(3, [src[s, x] for s in range(2) for x in range(CX)])
-    for chunk in range(2):
-        wait_recv(lambda a, b: x_copy(a, b, chunk), 0, (8, 9))
+    wait_recv(x_copy, 0, (8,))
     sign_y = jnp.where(lane == CY - 1, 1.0, jnp.where(lane == 0, -1.0, 0.0))
     on_y = sign_y != 0.0
     for x in range(CX):
@@ -636,15 +630,15 @@
             sign = -0.5 if x == 0 else 0.5
             missing = missing + 0.5 * kap[far, mid, :]
             face_x = 0.5 * (here + kap[far, mid, :])
-            drift_x = (-sign * velx[1 + x, mid, :], sign * velx[far, mid, :])
+            drift_x = -sign * velx[1 + x, mid, :]
         for s in range(2):
             scaled = missing if s == 0 else SCALES[s] * missing
             cof[0, s, 7, x] = cof[0, s, 7, x] - scaled
             bas[s, x] = bas[s, x] - scaled * fields[0, s, 1 + x, mid, :]
             for d in range(2):
                 cof[d, s, 6, x] = SCALES[s] * face_y + drift_y[d]
-                if x in (0, CX - 1):
-                    cof[d, s, 1 if x == 0 else 0, x] = SCALES[s] * face_x + drift_x[d]
+            if x in (0, CX - 1):
+                cof[0, s, 1 if x == 0 else 0, x] = SCALES[s] * face_x + drift_x
 
     whole = slice(0, NZ)
 
@@ -665,9 +659,8 @@
 
     def finish_all(slot, d, region, put, onward):
         halos = halo_planes(region, 2 * CX)
-        for chunk in range(4):
-            s, z = chunk // 2, chunk % 2
-            part = slice(z * PART, z * PART + PART)
+        for chunk in range(2):
+            s, part = chunk, whole
             wait_recv(lambda a, b: x_copy(a, b, chunk), 0, (slot,))
             for x in (0, CX - 1):
                 put(s, x, part, finish(slot, d, s, x, halos[s * CX + x], part))
@@ -682,15 +675,20 @@
 
     finish_all(0, 0, rim_f[0, mid, :], keep_base, 0)
 
-    for chunk in range(4):
-        s, z = chunk // 2, chunk % 2
-        part = slice(z * PART, z * PART + PART)
+    for chunk in range(2):
+        s, part = chunk, whole
         for x in (0, CX - 1):
             put_field(1, s, x, part, bas[s, x, part] + src[s, x, part])
         send_chunk(1, chunk)
     for s in range(2):
         for x in range(1, CX - 1):
             put_field(1, s, x, whole, bas[s, x] + src[s, x])
+
+    wait_recv(x_copy, 0, (9,))
+    for x, far, sign, f in ((0, 0, -0.5, 1), (CX - 1, CX + 1, 0.5, 0)):
+        face_x = 0.5 * (kap[1 + x, mid, :] + kap[far, mid, :])
+        for s in range(2):
+            cof[1, s, f, x] = SCALES[s] * face_x + sign * velx[far, mid, :]
 
     second = (lane & 32) != 0
     outside = ((lane < 64) & ((lane & 7) < 4) & (me_y == 0)) | (
@@ -759,7 +757,11 @@
         sen_of(t).wait_recv()
 
     for d in range(gxn):
-        sn2_o[d] = sen_i[pl.ds(d, gyn, stride=8), :]
+        held = sen_i[pl.ds(d, gyn, stride=8), :]
+        half = gyn // 2
+        sn2_o[d] = jnp.where(
+            iota((half, CY), 1) < 64, held[:half], pltpu.roll(held[half:], 64, 1)
+        )
 
     def sn2_copy(t, sending):
         there = lax.rem(me_x + t, gxn) if sending else lax.rem(me_x + gxn - t, gxn)
@@ -791,7 +793,8 @@
     def _(t):
         sn2_copy(t, False).wait_recv()
 
-    records = jnp.concatenate([sn2_i[d] for d in range(gxn)], axis=0)
+    both = jnp.concatenate([sn2_i[d] for d in range(gxn)], axis=0)
+    records = jnp.concatenate([both, pltpu.roll(both, 64, 1)], axis=0)
     many = records.shape[0]
     take = (iota((64, CY), 0) == iota((64, CY), 1)).astype(BF16)
     r0, r1, r2 = [dot_nt(take, part) for part in split3(records)]
@@ -888,15 +891,16 @@
         axis=0,
     )
     sums = []
+    q0, q1, q2 = [dot_nt(part, spots) for part in split3(stacked)]
+    picked = q0 + q1 + q2
     for s in range(2):
-        parts = split3(stacked[s * BZ * 32 : (s + 1) * BZ * 32])
         total = jnp.zeros((32, 2 * many_a), F32)
         for g in range(2):
-            q0, q1, q2 = [dot_nt(part, at_y[g]) for part in parts]
-            picked = q0 + q1 + q2
             part = jnp.zeros((32, 2 * many_a), F32)
+            span_g = slice(g * 2 * many_a, (g + 1) * 2 * many_a)
             for bz in range(BZ):
-                part = part + jnp.where(bz_row == bz, picked[bz * 32 : bz * 32 + 32], 0.0)
+                row = (s * BZ + bz) * 32
+                part = part + jnp.where(bz_row == bz, picked[row : row + 32, span_g], 0.0)
             total = total + foot_g[g] * part
         both = jnp.sum(total, axis=0, keepdims=True)
         sums.append(both + pltpu.roll(both, many_a, 1))
@@ -922,9 +926,7 @@
 
     both_sides(edge_copy, 1, wait_send, range(8))
     both_sides(x_copy, 0, wait_send, range(10))
-    both_sides(lambda a, b: x_copy(a, b, 1), 0, wait_send, range(10))
-    for chunk in range(2, 4):
-        both_sides(lambda a, b: x_copy(a, b, chunk), 0, wait_send, range(8))
+    both_sides(lambda a, b: x_copy(a, b, 1), 0, wait_send, range(8))
     both_sides(rim_copy, 0, wait_send, range(7))
 
     @pl.loop(1, gyn)
@@ -1023,8 +1025,8 @@
             pltpu.VMEM((rows, CY), F32),
             pltpu.VMEM((rows, CY), F32),
             pltpu.VMEM((rows, CY), F32),
-            pltpu.VMEM((gxn, gyn, CY), F32),
-            pltpu.VMEM((gxn, gyn, CY), F32),
+            pltpu.VMEM((gxn, gyn // 2, CY), F32),
+            pltpu.VMEM((gxn, gyn // 2, CY), F32),
             pltpu.VMEM((8, NZ // 2, CY), F32),
             pltpu.VMEM((8, NZ // 2, CY), F32),
             pltpu.VMEM((8, NZ // 2, CY), F32),
@@ -1034,8 +1036,8 @@
             pltpu.VMEM((8, CY), F32),
             pltpu.VMEM((rows, CY), F32),
             dma((12,)),
-            dma((10, 2, 4)),
-            dma((10, 2, 4)),
+            dma((10, 2, 2)),
+            dma((10, 2, 2)),
             dma((8, 2)),
             dma((8, 2)),
             dma((7, 2)),

time: 40.8 us -> 39.9 us (0.978)
  Pallas kernels: 40 us -> 39.1 us
    pallas_call x1, Pallas kernels: 39.2 us -> 38.4 us  [per_device(): pl.pallas_call(functools.partial(whole_kernel, gxn, gyn), out_shape=(pltp...]
where the time goes in v5:
time: 39.9 us; the launch traced here: 39.8 us
  Pallas kernels  39.1 us (98%)
  between operations  0.64 us (2%)
    pallas_call x1, Pallas kernels, per_device(): pl.pallas_call(functools.partial(whole_kernel, gxn, gyn), out_shape=(pltp...  38.4 us

profile of v5, /device:TPU:1, one launch (start us, length us, event | category | flops | bytes accessed | tf_op | source)
XLA Modules:
  0.0 39.8 jit_solution(17187739138220330462)
XLA Ops:
  0.6 38.4 %whole.1 = (f32[2,4,48,128]{3,2,1,0:T(8,128)S(1)}, f32[2,4,48,128]{3,2,1,0:T(8,128)S(1)}, f32[2,32]{1,0:T(2,128)S(1)}) custom-call(f32[2,4,48,128]{3,2,1,0:T(8,128)} %c0_h.1, f32[4,48,128]{2,1,0:T(8,128)} %kap_h.1, f32[3,4,48,128]{3,2,1,0:T(8,128)} %vel_h.1, f32[2,4,48,128]{3,2,1,0:T(8,128)} %tgt_h.1, s32[1,256]{1,0:T(1,128)} %bitcast.8, s32[1,256]{1,0:T(1,128)} %bitcast.9, ...), custom_call_target="tpu_custom_call" | custom-call | tf_op jit(solution)/shard_map/whole/pallas_call | solution.py:993
  39.0 0.8 %store.1 = (f32[2,4,48,128]{3,2,1,0:T(8,128)}, f32[2,4,48,128]{3,2,1,0:T(8,128)}, f32[2,32]{1,0:T(2,128)}) custom-call(f32[2,4,48,128]{3,2,1,0:T(8,128)S(1)} %get-tuple-element.9.state, f32[2,4,48,128]{3,2,1,0:T(8,128)S(1)} %get-tuple-element.10.sensitivity, f32[2,32]{1,0:T(2,128)S(1)} %get-tuple-element.11.gradient), custom_call_target="tpu_custom_call" | custom-call | tf_op jit(solution)/shard_map/store/pallas_call | solution.py:1071

commit v6 on v5

--- a/solution.py
+++ b/solution.py
@@ -910,8 +910,7 @@
         ]
     grad_o[...] = jnp.concatenate(sums + [jnp.zeros((6, CY), F32)], axis=0)
 
-    @pl.loop(1, gyn)
-    def _(t):
+    for t in far_first:
         grad_to(t).start()
 
     grad_i[own_tile, :] = grad_o[...]
@@ -938,12 +937,14 @@
     def _(t):
         sn2_copy(t, True).wait_send()
 
+    pick_lane = (iota((CY, acts), 0) == me_y * 4 + arank).astype(F32).astype(BF16)
+
     @pl.loop(1, gyn)
     def _(t):
         grad_of(t).wait_recv()
 
-    pick_lane = (iota((CY, acts), 0) == me_y * 4 + arank).astype(F32)
-    brought = dot_nn(grad_i[...], pick_lane, HIGH)
+    b0, b1, b2 = [dot_nn(part, pick_lane) for part in split3(grad_i[...])]
+    brought = b0 + b1 + b2
     mine = jnp.where(to_tile, brought, 0.0)
     for s in range(2):
         out_g[s : s + 1, :] = jnp.sum(

time: 39.9 us -> 39.7 us (level)
  no operation moved by 1% of the time
where the time goes in v6:
time: 39.7 us; the launch traced here: 39.6 us
  Pallas kernels  39 us (98%)
  between operations  0.64 us (2%)
    pallas_call x1, Pallas kernels, per_device(): pl.pallas_call(functools.partial(whole_kernel, gxn, gyn), out_shape=(pltp...  38.2 us

profile of v6, /device:TPU:1, one launch (start us, length us, event | category | flops | bytes accessed | tf_op | source)
XLA Modules:
  0.0 39.6 jit_solution(3315287039334032520)
XLA Ops:
  0.6 38.2 %whole.1 = (f32[2,4,48,128]{3,2,1,0:T(8,128)S(1)}, f32[2,4,48,128]{3,2,1,0:T(8,128)S(1)}, f32[2,32]{1,0:T(2,128)S(1)}) custom-call(f32[2,4,48,128]{3,2,1,0:T(8,128)} %c0_h.1, f32[4,48,128]{2,1,0:T(8,128)} %kap_h.1, f32[3,4,48,128]{3,2,1,0:T(8,128)} %vel_h.1, f32[2,4,48,128]{3,2,1,0:T(8,128)} %tgt_h.1, s32[1,256]{1,0:T(1,128)} %bitcast.8, s32[1,256]{1,0:T(1,128)} %bitcast.9, ...), custom_call_target="tpu_custom_call" | custom-call | tf_op jit(solution)/shard_map/whole/pallas_call | solution.py:994
  38.8 0.8 %store.1 = (f32[2,4,48,128]{3,2,1,0:T(8,128)}, f32[2,4,48,128]{3,2,1,0:T(8,128)}, f32[2,32]{1,0:T(2,128)}) custom-call(f32[2,4,48,128]{3,2,1,0:T(8,128)S(1)} %get-tuple-element.9.state, f32[2,4,48,128]{3,2,1,0:T(8,128)S(1)} %get-tuple-element.10.sensitivity, f32[2,32]{1,0:T(2,128)S(1)} %get-tuple-element.11.gradient), custom_call_target="tpu_custom_call" | custom-call | tf_op jit(solution)/shard_map/store/pallas_call | solution.py:1072
